TPU v7x, 256 devices: a whole 4x4x8 slice. The times are simulated.
256 devices in a mesh: sweep: 4 (over x_lo, core), cross: 64 (over y, z, x_hi).
Axes of the slice: x: 4 (x_hi: 2, x_lo: 2; x = x_hi * 2 + x_lo), y: 4, z: 8, core: 2. Of those that a mesh axis runs over, the one named last changes fastest.
Arguments:
- right_sides: bfloat16 [16, 512, 32, 135], P('sweep', 'cross'), may hold values from -0.099609375 to 0.099609375
- initial: bfloat16 [16, 512, 32, 135], P('sweep', 'cross'), may hold values from -0.099609375 to 0.099609375
- inverse_blocks: bfloat16 [16, 512, 135, 135], P('sweep', 'cross'), may hold values from -0.5 to 0.5
- couplings: bfloat16 [16, 512, 6, 45, 135], P('sweep', 'cross'), may hold values from -0.875 to 0.875
- neighbours: int32 [512, 4], P('cross'), may hold values from 0 to 511, as said below
Outputs:
- result: bfloat16 [16, 512, 32, 135], P('sweep', 'cross')
Inputs may be any that keep to these rules, and one draw needn't show every extreme that they name: `neighbours`: columns are numbered device by device along cross, 8 to a device. For a column with local index l on cross device k: face b- names column l of device k - 1 and face b+ column l of device k + 1 (cyclically); face c- names a column of device k - 1 or k, face c+ one of device k or k + 1.
All inputs are finite; a program needn't handle non-finite values.
Results may differ from a plain program's by a relative error of at most 0.029.
Values may be sent and summed in bfloat16 or wider, within the bound.
A program may use at most 64 MiB of HBM per device.

v0:
```python
import jax
import jax.numpy as jnp
from jax import lax
from jax.sharding import PartitionSpec as P

CROSS_FACES = ((1, 2), (1, 0), (2, 2), (2, 0))


def extended_2(cells, sides, width):
    for axis, dim in sides:
        count = lax.axis_size(axis)
        head = lax.slice_in_dim(cells, 0, width, axis=dim)
        tail = lax.slice_in_dim(cells, cells.shape[dim] - width, cells.shape[dim], axis=dim)
        cells = jnp.concatenate(
            [
                lax.ppermute(tail, axis, [(i, (i + 1) % count) for i in range(count)]),
                cells,
                lax.ppermute(head, axis, [((i + 1) % count, i) for i in range(count)]),
            ],
            axis=dim,
        )
    return cells


def passed_along(block, axis, distance):
    devices = range(lax.axis_size(axis))
    route = [(i - distance, i) for i in devices if i - distance in devices]
    return lax.ppermute(block, axis, route)


def selector(axis_place, which):
    slot = jnp.arange(45, dtype=jnp.int32)
    variable = slot // 9
    first = slot // 3 % 3
    second = slot % 3
    if axis_place == 0:
        target = variable * 27 + which * 9 + first * 3 + second
    elif axis_place == 1:
        target = variable * 27 + first * 9 + which * 3 + second
    else:
        target = variable * 27 + first * 9 + second * 3 + which
    unknown = jnp.arange(135, dtype=jnp.int32)[:, None]
    return (unknown == target[None, :]).astype(jnp.bfloat16)


def face_trace(field, axis_place, which):
    return jnp.dot(field, selector(axis_place, which), preferred_element_type=jnp.float32).astype(
        jnp.bfloat16
    )


def apply_faces(coupling, traces):
    return jnp.einsum("pcrt,pcti->pcri", traces, coupling, preferred_element_type=jnp.float32)


def cross_terms(field, couplings, neighbours):
    width = field.shape[1]
    place = lax.axis_index("cross")
    all_columns = width * lax.axis_size("cross")
    lower_which = (neighbours - (place - 1) * width) % all_columns
    total = jnp.zeros(field.shape, jnp.float32)
    extended = extended_2(field, (("cross", 1),), width)
    for face, (axis_place, which) in enumerate(CROSS_FACES):
        picked = jnp.take(extended, lower_which[:, face], axis=1)
        total = total + apply_faces(
            couplings[:, :, 2 + face], face_trace(picked, axis_place, which)
        )
    return total


def plane_chain(base, inverse, coupling, incoming, outgoing_face, backwards):
    count = base.shape[0]
    order = list(range(count))
    if backwards:
        order = order[::-1]
    solved_planes = {}
    trace_in = incoming
    for plane in order:
        term = jnp.einsum(
            "crt,cti->cri", trace_in, coupling[plane], preferred_element_type=jnp.float32
        )
        residue = (base[plane] - term).astype(jnp.bfloat16)
        solved = jnp.einsum(
            "crj,cij->cri", residue, inverse[plane], preferred_element_type=jnp.float32
        ).astype(jnp.bfloat16)
        solved_planes[plane] = solved
        trace_in = face_trace(solved, 0, outgoing_face)
    return (jnp.stack([solved_planes[plane] for plane in range(count)]), trace_in)


def chain_sections(base, inverse, coupling, outgoing_face, backwards, sender):
    sections = lax.axis_size("sweep")
    incoming = jnp.zeros((base.shape[1], base.shape[2], 45), jnp.bfloat16)
    solved = None
    for section in range(sections):
        solved, leaving = plane_chain(base, inverse, coupling, incoming, outgoing_face, backwards)
        if section + 1 < sections:
            incoming = sender(leaving)
    return (solved, incoming)


def run_chain(base, inverse, coupling, outgoing_face, backwards, direction):

    def sender(outgoing):
        return passed_along(outgoing, "sweep", direction)

    return chain_sections(base, inverse, coupling, outgoing_face, backwards, sender)


def local(right_sides, initial, inverse_blocks, couplings, neighbours):
    above = passed_along(face_trace(initial[0], 0, 0), "sweep", -1)
    upper_traces = jnp.concatenate([face_trace(initial[1:], 0, 0), above[None]], 0)
    forward_base = right_sides.astype(jnp.float32) - cross_terms(initial, couplings, neighbours)
    forward_base = forward_base - apply_faces(couplings[:, :, 1], upper_traces)
    middle, below = run_chain(forward_base, inverse_blocks, couplings[:, :, 0], 2, False, 1)
    lower_traces = jnp.concatenate([below[None], face_trace(middle[:-1], 0, 2)], 0)
    backward_base = right_sides.astype(jnp.float32) - cross_terms(middle, couplings, neighbours)
    backward_base = backward_base - apply_faces(couplings[:, :, 0], lower_traces)
    result, _unused = run_chain(backward_base, inverse_blocks, couplings[:, :, 1], 0, True, -1)
    return result


def solution(mesh):
    return jax.shard_map(
        local,
        mesh=mesh,
        in_specs=(
            P("sweep", "cross", None, None),
            P("sweep", "cross", None, None),
            P("sweep", "cross", None, None),
            P("sweep", "cross", None, None, None),
            P("cross", None),
        ),
        out_specs=P("sweep", "cross", None, None),
        check_vma=False,
    )
```

profile of v0, /device:TPU:1, one launch (start us, length us, event | category | flops | bytes accessed | tf_op | source)
XLA Modules:
  0.0 232.4 jit_solution(6398572596665014124)
XLA Ops:
  0.0 3.6 %collective-permute-start = (bf16[4,8,32,135]{3,2,1,0:T(8,128)(2,1)}, bf16[4,8,32,135]{3,2,1,0:T(8,128)(2,1)}, u32[]{:S(2)}, u32[]{:S(2)}) collective-permute-start(bf16[4,8,32,135]{3,2,1,0:T(8,128)(2,1)} %param.8), channel_id=1, source_target_pairs={{0,1},{1,2},{2,3},{3,4},{4,5},{5,6},{6,7},{7,8},{8,9},{9,10},{10,1... | collective-permute-start | bytes 829448 | tf_op jit(solution)/shard_map/ppermute | solution.py:16
  3.6 7.7 %collective-permute-start.1 = (bf16[4,8,32,135]{3,2,1,0:T(8,128)(2,1)}, bf16[4,8,32,135]{3,2,1,0:T(8,128)(2,1)}, u32[]{:S(2)}, u32[]{:S(2)}) collective-permute-start(bf16[4,8,32,135]{3,2,1,0:T(8,128)(2,1)} %param.8), channel_id=1, source_target_pairs={{1,0},{2,1},{3,2},{4,3},{5,4},{6,5},{7,6},{8,7},{9,8},{10,9},{11,1... | collective-permute-start | bytes 829448 | tf_op jit(solution)/shard_map/ppermute | solution.py:18
  13.1 2.8 %collective-permute-start.2 = (bf16[8,32,45]{2,1,0:T(8,128)(2,1)}, bf16[8,32,45]{2,1,0:T(8,128)(2,1)}, u32[]{:S(2)}, u32[]{:S(2)}) collective-permute-start(bf16[8,32,45]{2,1,0:T(8,128)(2,1)} %fusion.87), channel_id=1, source_target_pairs={{64,0},{128,64},{192,128},{65,1},{129,65},{193,129},{66,2},{130,66... | collective-permute-start | bytes 69128 | tf_op jit(solution)/shard_map/ppermute | solution.py:28
  16.6 2.0 fusion.36
  18.6 3.7 %fusion.275 = (bf16[4,8,1,45,135]{4,1,3,2,0:T(8,128)(2,1)}, bf16[4,8,1,45,135]{4,1,3,2,0:T(8,128)(2,1)}, bf16[4,8,1,45,135]{4,1,3,2,0:T(8,128)(2,1)S(1)}, bf16[4...) fusion(bf16[4,8,6,45,135]{4,1,3,2,0:T(8,128)(2,1)} %param.10), kind=kLoop, calls=%fused_computation.375 | loop fusion | bytes 4665600 | tf_op jit(solution)/shard_map/slice | solution.py:115
  22.3 2.9 %slice_bitcast_fusion.16 = (bf16[8,45,135]{2,0,1:T(8,128)(2,1)S(1)}, bf16[8,45,135]{2,0,1:T(8,128)(2,1)S(1)}, bf16[8,45,135]{2,0,1:T(8,128)(2,1)}, bf16[8,45,135...) fusion(bf16[4,8,6,45,135]{4,1,3,2,0:T(8,128)(2,1)} %param.10), kind=kLoop, calls=%fused_computation.234 | loop fusion | bytes 1555200 | tf_op jit(solution)/shard_map/squeeze | solution.py:80
  25.3 3.0 %fusion.276 = (bf16[1,8,135,135]{3,1,2,0:T(8,128)(2,1)}, bf16[1,8,135,135]{3,1,2,0:T(8,128)(2,1)}, bf16[1,8,135,135]{3,1,2,0:T(8,128)(2,1)}, bf16[1,8,135,135]{3,1,2,0:T(8,128)(2,1)}) fusion(bf16[4,8,135,135]{3,1,2,0:T(8,128)(2,1)} %param.9), kind=kLoop, calls=%fused_computation.376 | loop fusion | bytes 2332800 | tf_op jit(solution)/shard_map/slice | solution.py:84
  33.0 2.8 %gather_fusion = bf16[8,4,32,135]{3,2,1,0:T(8,128)(2,1)} fusion(bf16[4,24,32,135]{3,2,1,0:T(8,128)(2,1)} %constant_dynamic-update-slice_fusion, s32[1024]{0:T(1024)S(1)} %pad_clamp_fusion.3), kind=kCustom, calls=%fused_computation.clone | custom fusion | bytes 552992 | tf_op jit(solution)/shard_map/jit(_take)/gather | solution.py:64
  35.8 2.8 %gather_fusion.1 = bf16[8,4,32,135]{3,2,1,0:T(8,128)(2,1)} fusion(bf16[4,24,32,135]{3,2,1,0:T(8,128)(2,1)} %constant_dynamic-update-slice_fusion, s32[1024]{0:T(1024)S(1)} %pad_clamp_fusion.2), kind=kCustom, calls=%fused_computation.1.clone | custom fusion | bytes 552992 | tf_op jit(solution)/shard_map/jit(_take)/gather | solution.py:64
  38.6 2.8 %gather_fusion.2 = bf16[8,4,32,135]{3,2,1,0:T(8,128)(2,1)} fusion(bf16[4,24,32,135]{3,2,1,0:T(8,128)(2,1)} %constant_dynamic-update-slice_fusion, s32[1024]{0:T(1024)S(1)} %pad_clamp_fusion.1), kind=kCustom, calls=%fused_computation.2.clone | custom fusion | bytes 552992 | tf_op jit(solution)/shard_map/jit(_take)/gather | solution.py:64
  41.5 2.8 %gather_fusion.3 = bf16[8,4,32,135]{3,2,1,0:T(8,128)(2,1)} fusion(bf16[4,24,32,135]{3,2,1,0:T(8,128)(2,1)} %constant_dynamic-update-slice_fusion, s32[1024]{0:T(1024)S(1)} %pad_clamp_fusion), kind=kCustom, calls=%fused_computation.3.clone | custom fusion | bytes 552992 | tf_op jit(solution)/shard_map/jit(_take)/gather | solution.py:64
  44.2 2.6 %fusion.2 = f32[4,8,32,135]{3,2,1,0:T(8,128)} fusion(bf16[4,8,1,45,135]{4,1,3,2,0:T(8,128)(2,1)S(1)} %get-tuple-element.27, s32[45]{0:T(128)} %add_add_fusion.2, bf16[8,4,32,135]{3,2,1,0:T(8,128)(2,1)} %gather_fusion, pred[8]{0:T(512)(128)(4,1)S(1)} %get-tuple-element.36), kind=kOutput, calls=%fused_computation.61 | convolution fusion | flops 25073596 | bytes 1218428 | tf_op jit(solution)/shard_map/pcrt,pcti->pcri/dot_general | solution.py:53
  46.9 3.0 %convolution_add_fusion.5 = f32[4,8,32,135]{3,2,1,0:T(8,128)} fusion(f32[4,8,32,135]{3,2,1,0:T(8,128)} %fusion.2, bf16[4,8,1,45,135]{4,1,3,2,0:T(8,128)(2,1)S(1)} %get-tuple-element.26, s32[45]{0:T(128)S(1)} %fusion.269, bf16[8,4,32,135]{3,2,1,0:T(8,128)(2,1)} %gather_fusion.1, pred[8]{0:T(512)(128)(4,1)S(1)} %get-tuple-element.34), kind=kOutput, calls=%fused_computation.18 | convolution fusion | flops 25211836 | bytes 1771388 | tf_op jit(solution)/shard_map/pcrt,pcti->pcri/dot_general | solution.py:53
  49.8 3.0 %convolution_add_fusion.4 = f32[4,8,32,135]{3,2,1,0:T(8,128)} fusion(f32[4,8,32,135]{3,2,1,0:T(8,128)} %convolution_add_fusion.5, bf16[4,8,1,45,135]{4,1,3,2,0:T(8,128)(2,1)S(1)} %get-tuple-element.25, s32[45]{0:T(128)S(1)} %broadcast_add_fusion, bf16[8,4,32,135]{3,2,1,0:T(8,128)(2,1)} %gather_fusion.2, pred[8]{0:T(512)(128)(4,1)S(1)} %get-tuple-element.32), kind=kOutput, calls=%fused_computation.17 | convolution fusion | flops 25211836 | bytes 1771388 | tf_op jit(solution)/shard_map/pcrt,pcti->pcri/dot_general | solution.py:53
  52.9 3.0 %fusion.1 = f32[4,8,32,135]{3,2,1,0:T(8,128)} fusion(f32[4,8,32,135]{3,2,1,0:T(8,128)} %convolution_add_fusion.4, bf16[4,8,32,135]{3,2,1,0:T(8,128)(2,1)S(1)} %copy-done.13, bf16[4,8,1,45,135]{4,1,3,2,0:T(8,128)(2,1)S(1)} %get-tuple-element.24, s32[45]{0:T(128)S(1)} %multiply_add_fusion, bf16[8,4,32,135]{3,2,1,0:T(8,128)(2,1)} %gather_fusion.3, ...), kind=kOutput, calls=%fused_computation.16 | convolution fusion | flops 25488316 | bytes 2047868 | tf_op jit(solution)/shard_map/pcrt,pcti->pcri/dot_general | solution.py:53
  66.5 2.7 %collective-permute-start.3 = (bf16[8,32,45]{2,1,0:T(8,128)(2,1)S(1)}, bf16[8,32,45]{2,1,0:T(8,128)(2,1)S(1)}, u32[]{:S(2)}, u32[]{:S(2)}) collective-permute-start(bf16[8,32,45]{2,1,0:T(8,128)(2,1)S(1)} %fusion.83), channel_id=1, source_target_pairs={{0,64},{64,128},{128,192},{1,65},{65,129},{129,193},{2,66},{66,130... | collective-permute-start | bytes 69128 | tf_op jit(solution)/shard_map/ppermute | solution.py:28
  81.0 4.3 %collective-permute-start.4 = (bf16[8,32,45]{2,1,0:T(8,128)(2,1)S(1)}, bf16[8,32,45]{2,1,0:T(8,128)(2,1)S(1)}, u32[]{:S(2)}, u32[]{:S(2)}) collective-permute-start(bf16[8,32,45]{2,1,0:T(8,128)(2,1)S(1)} %fusion.79), channel_id=1, source_target_pairs={{0,64},{64,128},{128,192},{1,65},{65,129},{129,193},{2,66},{66,130... | collective-permute-start | bytes 69128 | tf_op jit(solution)/shard_map/ppermute | solution.py:28
  95.4 2.2 fusion.75
  97.6 4.3 %collective-permute-start.5 = (bf16[8,32,45]{2,1,0:T(8,128)(2,1)}, bf16[8,32,45]{2,1,0:T(8,128)(2,1)S(1)}, u32[]{:S(2)}, u32[]{:S(2)}) collective-permute-start(bf16[8,32,45]{2,1,0:T(8,128)(2,1)} %fusion.75), channel_id=1, source_target_pairs={{0,64},{64,128},{128,192},{1,65},{65,129},{129,193},{2,66},{66,130... | collective-permute-start | bytes 69128 | tf_op jit(solution)/shard_map/ppermute | solution.py:28
  103.5 2.2 convolution_convert_fusion.29
  107.4 2.1 convolution_convert_fusion.28
  111.3 2.1 convolution_convert_fusion.27
  115.3 2.1 fusion.49
  118.7 2.8 %collective-permute-start.6 = (bf16[4,8,32,135]{3,2,1,0:T(8,128)(2,1)S(1)}, bf16[4,8,32,135]{3,2,1,0:T(8,128)(2,1)S(1)}, u32[]{:S(2)}, u32[]{:S(2)}) collective-permute-start(bf16[4,8,32,135]{3,2,1,0:T(8,128)(2,1)S(1)} %pad_maximum_fusion.1), channel_id=1, source_target_pairs={{0,1},{1,2},{2,3},{3,4},{4,5},{5,6},{6,7},{7,8},{8,9},{9,10},{10,1... | collective-permute-start | bytes 829448 | tf_op jit(solution)/shard_map/ppermute | solution.py:16
  121.5 7.8 %collective-permute-start.7 = (bf16[4,8,32,135]{3,2,1,0:T(8,128)(2,1)S(1)}, bf16[4,8,32,135]{3,2,1,0:T(8,128)(2,1)S(1)}, u32[]{:S(2)}, u32[]{:S(2)}) collective-permute-start(bf16[4,8,32,135]{3,2,1,0:T(8,128)(2,1)S(1)} %pad_maximum_fusion.1), channel_id=1, source_target_pairs={{1,0},{2,1},{3,2},{4,3},{5,4},{6,5},{7,6},{8,7},{9,8},{10,9},{11,1... | collective-permute-start | bytes 829448 | tf_op jit(solution)/shard_map/ppermute | solution.py:18
  131.3 11.3 %collective-permute-done.6 = bf16[4,8,32,135]{3,2,1,0:T(8,128)(2,1)S(1)} collective-permute-done((bf16[4,8,32,135]{3,2,1,0:T(8,128)(2,1)S(1)}, bf16[4,8,32,135]{3,2,1,0:T(8,128)(2,1)S(1)}, u32[]{:S(2)}, u32[]{:S(2)}) %collective-permute-start.6) | collective-permute-done | bytes 276512 | tf_op jit(solution)/shard_map/ppermute | solution.py:16
  142.6 3.7 %collective-permute-done.7 = bf16[4,8,32,135]{3,2,1,0:T(8,128)(2,1)S(1)} collective-permute-done((bf16[4,8,32,135]{3,2,1,0:T(8,128)(2,1)S(1)}, bf16[4,8,32,135]{3,2,1,0:T(8,128)(2,1)S(1)}, u32[]{:S(2)}, u32[]{:S(2)}) %collective-permute-start.7) | collective-permute-done | bytes 276512 | tf_op jit(solution)/shard_map/ppermute | solution.py:18
  152.2 2.2 select_bitcast_fusion.2
  155.9 2.3 select_bitcast_fusion
  158.1 3.0 %convolution_add_fusion.2 = f32[4,8,32,135]{3,2,1,0:T(8,128)} fusion(f32[4,8,32,135]{3,2,1,0:T(8,128)} %fusion.3, bf16[4,8,1,45,135]{4,1,3,2,0:T(8,128)(2,1)S(1)} %copy-done.3, bf16[4,8,32,135]{3,2,0,1:T(8,128)(2,1)} %get-tuple-element.40, s32[45]{0:T(128)S(1)} %copy-done.27), kind=kOutput, calls=%fused_computation.13 | convolution fusion | flops 25073596 | bytes 1771380 | tf_op jit(solution)/shard_map/pcrt,pcti->pcri/dot_general | solution.py:53
  161.2 2.8 %convolution_add_fusion.1 = f32[4,8,32,135]{3,2,1,0:T(8,128)} fusion(f32[4,8,32,135]{3,2,1,0:T(8,128)} %convolution_add_fusion.2, bf16[4,8,1,45,135]{4,1,3,2,0:T(8,128)(2,1)S(1)} %copy-done.1, bf16[4,8,32,135]{3,2,0,1:T(8,128)(2,1)S(1)} %copy-done.21, s32[45]{0:T(128)S(1)} %broadcast_add_fusion), kind=kOutput, calls=%fused_computation.12 | convolution fusion | flops 25073596 | bytes 1771380 | tf_op jit(solution)/shard_map/pcrt,pcti->pcri/dot_general | solution.py:53
  164.0 1.9 fusion
  168.4 2.0 fusion.74
  172.1 2.0 fusion.73
  175.8 2.0 fusion.72
  179.4 2.0 fusion.71
  183.3 3.9 %collective-permute-done.8 = bf16[8,32,45]{2,1,0:T(8,128)(2,1)S(1)} collective-permute-done((bf16[8,32,45]{2,1,0:T(8,128)(2,1)}, bf16[8,32,45]{2,1,0:T(8,128)(2,1)S(1)}, u32[]{:S(2)}, u32[]{:S(2)}) %collective-permute-start.8) | collective-permute-done | bytes 23072 | tf_op jit(solution)/shard_map/ppermute | solution.py:28
  188.0 2.2 fusion.70
  191.8 1.9 fusion.69
  195.4 2.0 fusion.68
  199.0 2.0 fusion.67
  202.9 3.9 %collective-permute-done.9 = bf16[8,32,45]{2,1,0:T(8,128)(2,1)S(1)} collective-permute-done((bf16[8,32,45]{2,1,0:T(8,128)(2,1)}, bf16[8,32,45]{2,1,0:T(8,128)(2,1)S(1)}, u32[]{:S(2)}, u32[]{:S(2)}) %collective-permute-start.9) | collective-permute-done | bytes 23072 | tf_op jit(solution)/shard_map/ppermute | solution.py:28
  207.6 2.2 fusion.66
  211.4 1.9 fusion.65
  215.0 2.0 fusion.64
  218.7 1.9 fusion.63
  222.5 4.0 %collective-permute-done.10 = bf16[8,32,45]{2,1,0:T(8,128)(2,1)} collective-permute-done((bf16[8,32,45]{2,1,0:T(8,128)(2,1)}, bf16[8,32,45]{2,1,0:T(8,128)(2,1)}, u32[]{:S(2)}, u32[]{:S(2)}) %collective-permute-start.10) | collective-permute-done | bytes 23072 | tf_op jit(solution)/shard_map/ppermute | solution.py:28
  226.5 2.1 convolution_convert_fusion.13
  (144 shorter events, 85.8 us)
Async XLA Ops:
  0.0 28.4 %collective-permute-start = (bf16[4,8,32,135]{3,2,1,0:T(8,128)(2,1)}, bf16[4,8,32,135]{3,2,1,0:T(8,128)(2,1)}, u32[]{:S(2)}, u32[]{:S(2)}) collective-permute-start(bf16[4,8,32,135]{3,2,1,0:T(8,128)(2,1)} %param.8), channel_id=1, source_target_pairs={{0,1},{1,2},{2,3},{3,4},{4,5},{5,6},{6,7},{7,8},{8,9},{9,10},{10,1... | collective-permute-start | bytes 829448 | tf_op jit(solution)/shard_map/ppermute | solution.py:16
  3.6 27.6 %collective-permute-start.1 = (bf16[4,8,32,135]{3,2,1,0:T(8,128)(2,1)}, bf16[4,8,32,135]{3,2,1,0:T(8,128)(2,1)}, u32[]{:S(2)}, u32[]{:S(2)}) collective-permute-start(bf16[4,8,32,135]{3,2,1,0:T(8,128)(2,1)} %param.8), channel_id=1, source_target_pairs={{1,0},{2,1},{3,2},{4,3},{5,4},{6,5},{7,6},{8,7},{9,8},{10,9},{11,1... | collective-permute-start | bytes 829448 | tf_op jit(solution)/shard_map/ppermute | solution.py:18
  13.1 42.8 %collective-permute-start.2 = (bf16[8,32,45]{2,1,0:T(8,128)(2,1)}, bf16[8,32,45]{2,1,0:T(8,128)(2,1)}, u32[]{:S(2)}, u32[]{:S(2)}) collective-permute-start(bf16[8,32,45]{2,1,0:T(8,128)(2,1)} %fusion.87), channel_id=1, source_target_pairs={{64,0},{128,64},{192,128},{65,1},{129,65},{193,129},{66,2},{130,66... | collective-permute-start | bytes 69128 | tf_op jit(solution)/shard_map/ppermute | solution.py:28
  16.6 30.3 %copy-start.26 = (s32[45]{0:T(128)}, s32[45]{0:T(128)S(1)}, u32[]{:S(2)}) copy-start(s32[45]{0:T(128)S(1)} %fusion.269) | copy-start | bytes 544
  22.3 24.6 %copy-start.2 = (bf16[4,8,1,45,135]{4,1,3,2,0:T(8,128)(2,1)}, bf16[4,8,1,45,135]{4,1,3,2,0:T(8,128)(2,1)S(1)}, u32[]{:S(2)}) copy-start(bf16[4,8,1,45,135]{4,1,3,2,0:T(8,128)(2,1)S(1)} %get-tuple-element.26) | copy-start | bytes 1166404
  22.3 27.6 %copy-start = (bf16[4,8,1,45,135]{4,1,3,2,0:T(8,128)(2,1)}, bf16[4,8,1,45,135]{4,1,3,2,0:T(8,128)(2,1)S(1)}, u32[]{:S(2)}) copy-start(bf16[4,8,1,45,135]{4,1,3,2,0:T(8,128)(2,1)S(1)} %get-tuple-element.25) | copy-start | bytes 1166404
  22.3 2.9 %copy-start.30 = (s32[8,4]{0,1:T(4,128)S(1)}, s32[8,4]{0,1:T(4,128)}, u32[]{:S(2)}) copy-start(s32[8,4]{0,1:T(4,128)} %param.11) | copy-start | bytes 388
  25.3 5.0 %copy-start.24 = (bf16[4,8,32,135]{3,2,1,0:T(8,128)(2,1)S(1)}, bf16[4,8,32,135]{3,2,1,0:T(8,128)(2,1)}, u32[]{:S(2)}) copy-start(bf16[4,8,32,135]{3,2,1,0:T(8,128)(2,1)} %param.8) | copy-start | bytes 829444
  28.3 24.5 %copy-start.28 = (s32[45]{0:T(128)}, s32[45]{0:T(128)S(1)}, u32[]{:S(2)}) copy-start(s32[45]{0:T(128)S(1)} %multiply_add_fusion) | copy-start | bytes 544
  49.8 3.0 %copy-start.13 = (bf16[4,8,32,135]{3,2,1,0:T(8,128)(2,1)S(1)}, bf16[4,8,32,135]{3,2,1,0:T(8,128)(2,1)}, u32[]{:S(2)}) copy-start(bf16[4,8,32,135]{3,2,1,0:T(8,128)(2,1)} %param.7) | copy-start | bytes 829444
  52.9 3.0 %copy-start.25 = (bf16[3,8,32,45]{3,2,1,0:T(8,128)(2,1)S(1)}, bf16[3,8,32,45]{3,2,1,0:T(8,128)(2,1)}, u32[]{:S(2)}) copy-start(bf16[3,8,32,45]{3,2,1,0:T(8,128)(2,1)} %fusion.36) | copy-start | bytes 207364
  55.9 1.8 copy-start.8
  57.7 4.0 %copy-start.7 = (bf16[8,45,135]{2,0,1:T(8,128)(2,1)S(1)}, bf16[8,45,135]{2,0,1:T(8,128)(2,1)}, u32[]{:S(2)}) copy-start(bf16[8,45,135]{2,0,1:T(8,128)(2,1)} %get-tuple-element.18) | copy-start | bytes 291604
  59.4 4.8 %copy-start.6 = (bf16[8,45,135]{2,0,1:T(8,128)(2,1)S(1)}, bf16[8,45,135]{2,0,1:T(8,128)(2,1)}, u32[]{:S(2)}) copy-start(bf16[8,45,135]{2,0,1:T(8,128)(2,1)} %get-tuple-element.17) | copy-start | bytes 291604
  66.5 4.0 %collective-permute-start.3 = (bf16[8,32,45]{2,1,0:T(8,128)(2,1)S(1)}, bf16[8,32,45]{2,1,0:T(8,128)(2,1)S(1)}, u32[]{:S(2)}, u32[]{:S(2)}) collective-permute-start(bf16[8,32,45]{2,1,0:T(8,128)(2,1)S(1)} %fusion.83), channel_id=1, source_target_pairs={{0,64},{64,128},{128,192},{1,65},{65,129},{129,193},{2,66},{66,130... | collective-permute-start | bytes 69128 | tf_op jit(solution)/shard_map/ppermute | solution.py:28
  81.0 5.6 %collective-permute-start.4 = (bf16[8,32,45]{2,1,0:T(8,128)(2,1)S(1)}, bf16[8,32,45]{2,1,0:T(8,128)(2,1)S(1)}, u32[]{:S(2)}, u32[]{:S(2)}) collective-permute-start(bf16[8,32,45]{2,1,0:T(8,128)(2,1)S(1)} %fusion.79), channel_id=1, source_target_pairs={{0,64},{64,128},{128,192},{1,65},{65,129},{129,193},{2,66},{66,130... | collective-permute-start | bytes 69128 | tf_op jit(solution)/shard_map/ppermute | solution.py:28
  97.6 5.9 %collective-permute-start.5 = (bf16[8,32,45]{2,1,0:T(8,128)(2,1)}, bf16[8,32,45]{2,1,0:T(8,128)(2,1)S(1)}, u32[]{:S(2)}, u32[]{:S(2)}) collective-permute-start(bf16[8,32,45]{2,1,0:T(8,128)(2,1)} %fusion.75), channel_id=1, source_target_pairs={{0,64},{64,128},{128,192},{1,65},{65,129},{129,193},{2,66},{66,130... | collective-permute-start | bytes 69128 | tf_op jit(solution)/shard_map/ppermute | solution.py:28
  109.5 7.9 %copy-start.15 = (bf16[8,32,135]{2,1,0:T(8,128)(2,1)S(1)}, bf16[8,32,135]{2,1,0:T(8,128)(2,1)}, u32[]{:S(2)}) copy-start(bf16[8,32,135]{2,1,0:T(8,128)(2,1)} %convolution_convert_fusion.29) | copy-start | bytes 207364
  113.5 15.8 %copy-start.17 = (bf16[8,32,135]{2,1,0:T(8,128)(2,1)S(1)}, bf16[8,32,135]{2,1,0:T(8,128)(2,1)}, u32[]{:S(2)}) copy-start(bf16[8,32,135]{2,1,0:T(8,128)(2,1)} %convolution_convert_fusion.28) | copy-start | bytes 207364
  117.4 28.8 %copy-start.16 = (bf16[8,32,135]{2,1,0:T(8,128)(2,1)S(1)}, bf16[8,32,135]{2,1,0:T(8,128)(2,1)}, u32[]{:S(2)}) copy-start(bf16[8,32,135]{2,1,0:T(8,128)(2,1)} %convolution_convert_fusion.29) | copy-start | bytes 207364
  117.4 28.8 %copy-start.18 = (bf16[8,32,135]{2,1,0:T(8,128)(2,1)S(1)}, bf16[8,32,135]{2,1,0:T(8,128)(2,1)}, u32[]{:S(2)}) copy-start(bf16[8,32,135]{2,1,0:T(8,128)(2,1)} %convolution_convert_fusion.28) | copy-start | bytes 207364
  117.4 28.8 %copy-start.19 = (bf16[8,32,135]{2,1,0:T(8,128)(2,1)S(1)}, bf16[8,32,135]{2,1,0:T(8,128)(2,1)}, u32[]{:S(2)}) copy-start(bf16[8,32,135]{2,1,0:T(8,128)(2,1)} %convolution_convert_fusion.27) | copy-start | bytes 207364
  117.4 28.8 %copy-start.22 = (bf16[1,8,32,135]{3,2,1,0:T(8,128)(2,1)S(1)}, bf16[1,8,32,135]{3,2,1,0:T(8,128)(2,1)}, u32[]{:S(2)}) copy-start(bf16[1,8,32,135]{3,2,1,0:T(8,128)(2,1)} %fusion.49) | copy-start | bytes 207364
  118.7 23.9 %collective-permute-start.6 = (bf16[4,8,32,135]{3,2,1,0:T(8,128)(2,1)S(1)}, bf16[4,8,32,135]{3,2,1,0:T(8,128)(2,1)S(1)}, u32[]{:S(2)}, u32[]{:S(2)}) collective-permute-start(bf16[4,8,32,135]{3,2,1,0:T(8,128)(2,1)S(1)} %pad_maximum_fusion.1), channel_id=1, source_target_pairs={{0,1},{1,2},{2,3},{3,4},{4,5},{5,6},{6,7},{7,8},{8,9},{9,10},{10,1... | collective-permute-start | bytes 829448 | tf_op jit(solution)/shard_map/ppermute | solution.py:16
  121.5 24.7 %collective-permute-start.7 = (bf16[4,8,32,135]{3,2,1,0:T(8,128)(2,1)S(1)}, bf16[4,8,32,135]{3,2,1,0:T(8,128)(2,1)S(1)}, u32[]{:S(2)}, u32[]{:S(2)}) collective-permute-start(bf16[4,8,32,135]{3,2,1,0:T(8,128)(2,1)S(1)} %pad_maximum_fusion.1), channel_id=1, source_target_pairs={{1,0},{2,1},{3,2},{4,3},{5,4},{6,5},{7,6},{8,7},{9,8},{10,9},{11,1... | collective-permute-start | bytes 829448 | tf_op jit(solution)/shard_map/ppermute | solution.py:18
  150.8 3.5 %copy-start.31 = (s32[45]{0:T(128)S(1)}, s32[45]{0:T(128)}, u32[]{:S(2)}) copy-start(s32[45]{0:T(128)} %add_add_fusion.2) | copy-start | bytes 544
  154.3 1.5 copy-start.20
  155.9 2.3 copy-start.3
  155.9 2.3 copy-start.27
  158.1 3.0 %copy-start.1 = (bf16[4,8,1,45,135]{4,1,3,2,0:T(8,128)(2,1)S(1)}, bf16[4,8,1,45,135]{4,1,3,2,0:T(8,128)(2,1)}, u32[]{:S(2)}) copy-start(bf16[4,8,1,45,135]{4,1,3,2,0:T(8,128)(2,1)} %copy-done) | copy-start | bytes 1166404
  158.1 3.0 %copy-start.21 = (bf16[4,8,32,135]{3,2,0,1:T(8,128)(2,1)S(1)}, bf16[4,8,32,135]{3,2,0,1:T(8,128)(2,1)}, u32[]{:S(2)}) copy-start(bf16[4,8,32,135]{3,2,0,1:T(8,128)(2,1)} %get-tuple-element.39) | copy-start | bytes 829444
  161.2 2.8 %copy-start.14 = (bf16[4,8,32,135]{3,2,1,0:T(8,128)(2,1)S(1)}, bf16[4,8,32,135]{3,2,1,0:T(8,128)(2,1)}, u32[]{:S(2)}) copy-start(bf16[4,8,32,135]{3,2,1,0:T(8,128)(2,1)} %param.7) | copy-start | bytes 829444
  161.2 2.8 %copy-start.29 = (s32[45]{0:T(128)S(1)}, s32[45]{0:T(128)}, u32[]{:S(2)}) copy-start(s32[45]{0:T(128)} %copy-done.28) | copy-start | bytes 544
  165.9 1.6 copy-start.5
  166.0 2.5 %copy-start.12 = (bf16[1,8,135,135]{3,1,2,0:T(8,128)(2,1)S(1)}, bf16[1,8,135,135]{3,1,2,0:T(8,128)(2,1)}, u32[]{:S(2)}) copy-start(bf16[1,8,135,135]{3,1,2,0:T(8,128)(2,1)} %get-tuple-element.28) | copy-start | bytes 874804
  166.0 4.5 %copy-start.4 = (bf16[8,45,135]{2,0,1:T(8,128)(2,1)S(1)}, bf16[8,45,135]{2,0,1:T(8,128)(2,1)}, u32[]{:S(2)}) copy-start(bf16[8,45,135]{2,0,1:T(8,128)(2,1)} %get-tuple-element.20) | copy-start | bytes 291604
  167.6 4.5 %copy-start.11 = (bf16[1,8,135,135]{3,1,2,0:T(8,128)(2,1)S(1)}, bf16[1,8,135,135]{3,1,2,0:T(8,128)(2,1)}, u32[]{:S(2)}) copy-start(bf16[1,8,135,135]{3,1,2,0:T(8,128)(2,1)} %get-tuple-element.29) | copy-start | bytes 874804
  168.4 7.4 %copy-start.10 = (bf16[1,8,135,135]{3,1,2,0:T(8,128)(2,1)S(1)}, bf16[1,8,135,135]{3,1,2,0:T(8,128)(2,1)}, u32[]{:S(2)}) copy-start(bf16[1,8,135,135]{3,1,2,0:T(8,128)(2,1)} %get-tuple-element.30) | copy-start | bytes 874804
  172.1 7.3 %copy-start.9 = (bf16[1,8,135,135]{3,1,2,0:T(8,128)(2,1)S(1)}, bf16[1,8,135,135]{3,1,2,0:T(8,128)(2,1)}, u32[]{:S(2)}) copy-start(bf16[1,8,135,135]{3,1,2,0:T(8,128)(2,1)} %get-tuple-element.31) | copy-start | bytes 874804
  181.4 5.8 %collective-permute-start.8 = (bf16[8,32,45]{2,1,0:T(8,128)(2,1)}, bf16[8,32,45]{2,1,0:T(8,128)(2,1)S(1)}, u32[]{:S(2)}, u32[]{:S(2)}) collective-permute-start(bf16[8,32,45]{2,1,0:T(8,128)(2,1)} %fusion.71), channel_id=1, source_target_pairs={{64,0},{128,64},{192,128},{65,1},{129,65},{193,129},{66,2},{130,66... | collective-permute-start | bytes 69128 | tf_op jit(solution)/shard_map/ppermute | solution.py:28
  201.0 5.8 %collective-permute-start.9 = (bf16[8,32,45]{2,1,0:T(8,128)(2,1)}, bf16[8,32,45]{2,1,0:T(8,128)(2,1)S(1)}, u32[]{:S(2)}, u32[]{:S(2)}) collective-permute-start(bf16[8,32,45]{2,1,0:T(8,128)(2,1)} %fusion.67), channel_id=1, source_target_pairs={{64,0},{128,64},{192,128},{65,1},{129,65},{193,129},{66,2},{130,66... | collective-permute-start | bytes 69128 | tf_op jit(solution)/shard_map/ppermute | solution.py:28
  220.6 5.9 %collective-permute-start.10 = (bf16[8,32,45]{2,1,0:T(8,128)(2,1)}, bf16[8,32,45]{2,1,0:T(8,128)(2,1)}, u32[]{:S(2)}, u32[]{:S(2)}) collective-permute-start(bf16[8,32,45]{2,1,0:T(8,128)(2,1)} %fusion.63), channel_id=1, source_target_pairs={{64,0},{128,64},{192,128},{65,1},{129,65},{193,129},{66,2},{130,66... | collective-permute-start | bytes 69128 | tf_op jit(solution)/shard_map/ppermute | solution.py:28
  230.2 1.3 copy-start.23
where the time goes:
time: 234 us; the launch traced here: 232 us
  matrix products  121 us (52%)
  starting transfers between devices  41.8 us (18%)
  local copies, waits for them, and re-layouts  31.1 us (13%)
  waiting for transfers between devices  30.9 us (13%)
  other arithmetic  7.65 us (3%)
    dot_general x33, matrix products, face_trace(): jnp.dot(field, selector(axis_place, which), preferred_element_type=jnp.fl...  55.6 us
    dot_general x24, matrix products, plane_chain(): jnp.einsum('crt,cti->cri', trace_in, coupling[plane], preferred_element_t...  28.6 us
    dot_general x10, matrix products, apply_faces(): jnp.einsum('pcrt,pcti->pcri', traces, coupling, preferred_element_type=jn...  24.4 us
    ppermute x7, starting transfers between devices, passed_along(): return lax.ppermute(block, axis, route)  19.8 us
    gather x8, local copies, waits for them, and re-layouts, cross_terms(): picked = jnp.take(extended, lower_which[:, face], axis=1)  16.7 us
    ppermute x7, waiting for transfers between devices, passed_along(): return lax.ppermute(block, axis, route)  16 us
    ppermute x2, starting transfers between devices, extended_2(): lax.ppermute(head, axis, [((i + 1) % count, i) for i in range(count)])  15.6 us
    dot_general x8, matrix products, plane_chain(): jnp.einsum('crj,cij->cri', residue, inverse[plane], preferred_element_typ...  11.9 us
  transfers between devices with their start and end apart: 11, of which 8 were waited for; matrix products, arithmetic and copies ran while one was open for 19% of the time, Pallas kernels for 0%

commit v1 on v0

v1 whole, which is shorter than its diff:
```python
import functools

import jax
import jax.numpy as jnp
import numpy as np
from jax import lax
from jax.experimental import pallas as pl
from jax.experimental.pallas import tpu as pltpu
from jax.sharding import PartitionSpec as P

MESH = pl.DeviceIdType.MESH
NU, NT, R, CC, NP = 135, 45, 32, 8, 4
FT = 48
LANES = NP * R
F32, BF16 = jnp.float32, jnp.bfloat16
FACES = ((1, 2), (2, 2), (1, 0), (2, 0), (0, 0), (0, 2))
STACK = (1, 2, 3, 4, 5)
NSTACK = len(STACK) * FT
LOWER = 256


def selector():
    rows = np.zeros((len(FACES) * FT, NU), np.float32)
    for face, (axis_place, which) in enumerate(FACES):
        for slot in range(NT):
            v, first, second = slot // 9, slot // 3 % 3, slot % 3
            node = [first, second]
            node.insert(axis_place, which)
            rows[face * FT + slot, v * 27 + node[0] * 9 + node[1] * 3 + node[2]] = 1.0
    return rows


def nn(a, b):
    return lax.dot_general(a, b, (((1,), (0,)), ((), ())), preferred_element_type=F32)


def nt(a, b):
    return lax.dot_general(a, b, (((1,), (1,)), ((), ())), preferred_element_type=F32)


def blocks(rows):
    return lax.broadcasted_iota(jnp.int32, (rows, LANES), 1) // R


def by_block(rows, parts):
    block = blocks(rows)
    total = jnp.zeros((rows, LANES), F32)
    for b, part in parts:
        total = jnp.where(block == b, part, total)
    return total


def kernel(
    crosses,
    neigh,
    sel,
    rhs_hbm,
    init_hbm,
    inv_hbm,
    cpl_hbm,
    out_hbm,
    init_v,
    rhs_v,
    inv_v,
    cpl_v,
    out_v,
    stack_v,
    d_v,
    w_v,
    x_v,
    v_v,
    m_v,
    u_v,
    us_v,
    q_v,
    e_v,
    ext_l0,
    ext_l1,
    ext_r0,
    ext_r1,
    up_s,
    up_r,
    a_s,
    a_r,
    m_s,
    m_r,
    load_sem,
    col_sem,
    out_sem,
    halo_s,
    halo_r,
    upsem,
    a_ss,
    a_rs,
    m_ss,
    m_rs,
):
    ext_l, ext_r = (ext_l0, ext_l1), (ext_r0, ext_r1)
    s = lax.axis_index("sweep")
    k = lax.axis_index("cross")
    right = lax.rem(k + 1, crosses)
    left = lax.rem(k + crosses - 1, crosses)

    load_init = pltpu.make_async_copy(init_hbm, init_v, load_sem.at[0])
    load_rhs = pltpu.make_async_copy(rhs_hbm, rhs_v, load_sem.at[1])
    load_init.start()
    load_rhs.start()

    def inv_load(c):
        return pltpu.make_async_copy(inv_hbm.at[:, c], inv_v.at[:, c], col_sem.at[0, c])

    def cpl_load(c):
        return pltpu.make_async_copy(cpl_hbm.at[:, c], cpl_v.at[:, c], col_sem.at[1, c])

    for c in range(CC):
        inv_load(c).start()
        cpl_load(c).start()

    barrier = pltpu.get_barrier_semaphore()
    for other in (left, right):
        pl.semaphore_signal(barrier, inc=1, device_id={"cross": other}, device_id_type=MESH)
    for step in (1, 2, 3):
        pl.semaphore_signal(
            barrier, inc=1, device_id={"sweep": lax.rem(s + step, 4)}, device_id_type=MESH
        )

    stack_v[...] = jnp.zeros_like(stack_v)
    u_v[...] = jnp.zeros_like(u_v)

    @pl.when(s == 3)
    def _():
        up_r[...] = jnp.zeros_like(up_r)

    for step in (1, 2, 3):

        @pl.when(s < step)
        def _():
            a_r[0, step - 1] = jnp.zeros((FT, CC * R), BF16)

        @pl.when(s + step > 3)
        def _():
            a_r[1, step - 1] = jnp.zeros((FT, CC * R), BF16)

    for step in (1, 2):

        @pl.when(s < step + 1)
        def _():
            m_r[0, step - 1] = jnp.zeros((CC, FT, FT), BF16)

        @pl.when(s + step > 2)
        def _():
            m_r[1, step - 1] = jnp.zeros((CC, FT, FT), BF16)

    load_init.wait()
    up_s[...] = nt(sel[4 * FT : 5 * FT], init_v[0].reshape(CC * R, NU)).astype(BF16)

    def first_traces(g, carry):
        for b in range(4):
            c = 4 * g + b
            picked = nt(sel[0 : 5 * FT], init_v[:, c].reshape(LANES, NU))
            ext_l[0][CC + c] = picked[0 : 2 * FT].astype(BF16)
            ext_r[0][c] = picked[2 * FT : 4 * FT].astype(BF16)
            us_v[c] = pltpu.roll(picked[4 * FT : 5 * FT], LANES - R, 1)
        return carry

    lax.fori_loop(0, 2, first_traces, 0)
    pl.semaphore_wait(barrier, 5)

    def halo(sweep):
        return (
            pltpu.make_async_remote_copy(
                ext_l[sweep].at[pl.ds(CC, CC)],
                ext_l[sweep].at[pl.ds(0, CC)],
                halo_s.at[sweep, 0],
                halo_r.at[sweep, 0],
                device_id={"cross": right},
                device_id_type=MESH,
            ),
            pltpu.make_async_remote_copy(
                ext_r[sweep].at[pl.ds(0, CC)],
                ext_r[sweep].at[pl.ds(CC, CC)],
                halo_s.at[sweep, 1],
                halo_r.at[sweep, 1],
                device_id={"cross": left},
                device_id_type=MESH,
            ),
        )

    up_copy = pltpu.make_async_remote_copy(
        up_s,
        up_r,
        upsem.at[0],
        upsem.at[1],
        device_id={"sweep": lax.rem(s + 3, 4)},
        device_id_type=MESH,
    )
    for copy in halo(0):
        copy.start()

    @pl.when(s > 0)
    def _():
        up_copy.start()

    def a_copy(sweep, step):
        to = lax.rem(s + step, 4) if sweep == 0 else lax.rem(s + 4 - step, 4)
        return pltpu.make_async_remote_copy(
            a_s.at[sweep],
            a_r.at[sweep, step - 1],
            a_ss.at[sweep, step - 1],
            a_rs.at[sweep, step - 1],
            device_id={"sweep": to},
            device_id_type=MESH,
        )

    def m_copy(sweep, step):
        to = lax.rem(s + step, 4) if sweep == 0 else lax.rem(s + 4 - step, 4)
        return pltpu.make_async_remote_copy(
            m_s.at[sweep],
            m_r.at[sweep, step - 1],
            m_ss.at[sweep, step - 1],
            m_rs.at[sweep, step - 1],
            device_id={"sweep": to},
            device_id_type=MESH,
        )

    def a_sends(sweep, step):
        return s + step < 4 if sweep == 0 else s >= step

    def a_takes(sweep, step):
        return s >= step if sweep == 0 else s + step < 4

    def m_sends(sweep, step):
        if sweep == 0:
            return jnp.logical_and(s >= 1, s + step < 4)
        return jnp.logical_and(s <= 2, s >= step)

    def m_takes(sweep, step):
        return s >= step + 1 if sweep == 0 else s + step <= 2

    load_rhs.wait()

    def products(g, carry):
        for b in range(4):
            c = 4 * g + b
            inv_load(c).wait()
            cpl_load(c).wait()
            for p in range(NP):
                for place, face in enumerate(STACK):
                    stack_v[p, FT * place : FT * place + NT] = cpl_v[p, c, face]
                stack_v[p, LOWER : LOWER + NT] = cpl_v[p, c, 0]
                d_v[p, c] = nt(inv_v[p, c], stack_v[p]).astype(BF16)
            rhs = rhs_v[:, c].reshape(LANES, NU)
            w_v[c] = by_block(NU, [(p, nt(inv_v[p, c], rhs)) for p in range(NP)])
        return carry

    lax.fori_loop(0, 2, products, 0)

    def d_in(sweep, p, c):
        if sweep == 0:
            return d_v[p, c, :, LOWER : LOWER + FT]
        return d_v[p, c, :, 0:FT]

    def sections(sweep):
        order = range(NP) if sweep == 0 else range(NP - 1, -1, -1)
        rows = sel[5 * FT : 6 * FT] if sweep == 0 else sel[4 * FT : 5 * FT]

        def body(g, carry):
            for b in range(4):
                c = 4 * g + b
                before = None
                for p in order:
                    d = d_in(sweep, p, c)
                    q = nn(rows, d).astype(BF16)
                    q_v[sweep, c, p] = q
                    if before is None:
                        e_v[sweep, c, p] = d
                        before = -q
                    else:
                        e_v[sweep, c, p] = nn(d, before).astype(BF16)
                        before = (-nn(q, before)).astype(BF16)
                m_s[sweep, c] = before
            return carry

        lax.fori_loop(0, 2, body, 0)
        for step in (1, 2):

            @pl.when(m_sends(sweep, step))
            def _():
                m_copy(sweep, step).start()

    sections(0)

    def gathered(sweep, c, upper):
        low = lax.rem(neigh[c, 2] - (k - 1) * CC + 2 * crosses * CC, crosses * CC)
        high = lax.rem(neigh[c, 3] - k * CC + crosses * CC, crosses * CC)
        low = jnp.clip(low, 0, 2 * CC - 1)
        high = jnp.clip(high, 0, 2 * CC - 1)
        return jnp.concatenate(
            [
                upper,
                ext_l[sweep][c, 0:FT],
                ext_r[sweep][CC + c, 0:FT],
                ext_l[sweep][low, FT : 2 * FT],
                ext_r[sweep][high, FT : 2 * FT],
            ],
            axis=0,
        )

    def local_sweep(sweep, c, base, upper):
        order = list(range(NP)) if sweep == 0 else list(range(NP - 1, -1, -1))
        shift = R if sweep == 0 else LANES - R
        stack = gathered(sweep, c, upper)
        x = by_block(NU, [(p, nn(d_v[p, c, :, 0:NSTACK], stack)) for p in range(NP)])
        v = base - x
        v_v[c] = v
        if sweep == 0:
            x_v[c] = x
        start = 18 if sweep == 0 else 0
        for var in range(5):
            u_v[c, 9 * var : 9 * var + 9] = v_v[c, 27 * var + start : 27 * var + start + 9]
        u = u_v[c]
        block = blocks(FT)
        now = u
        for p in order[1:]:
            z = nn(q_v[sweep, c, p], pltpu.roll(now, shift, 1).astype(BF16))
            now = jnp.where(block == p, u - z, now)
        before = jnp.where(block == order[0], 0.0, pltpu.roll(now, shift, 1)).astype(BF16)
        y = by_block(NU, [(p, nn(d_in(sweep, p, c), before)) for p in order[1:]])
        m_v[c] = v - y
        return now

    def packed(sweep, c, b, now, total):
        last = 3 if sweep == 0 else 0
        turned = now if b == last else pltpu.roll(now, (R * (b - last)) % LANES, 1)
        return jnp.where(blocks(FT) == b, turned, total)

    def spread(b, group):
        one = jnp.where(blocks(FT) == b, group, 0.0)
        one = one + pltpu.roll(one, R, 1)
        return (one + pltpu.roll(one, 2 * R, 1)).astype(BF16)

    def send_ends(sweep):
        for step in (1, 2, 3):

            @pl.when(a_sends(sweep, step))
            def _():
                a_copy(sweep, step).start()

    def take_ends(sweep):
        for step in (1, 2, 3):

            @pl.when(a_takes(sweep, step))
            def _():
                a_copy(sweep, step).wait_recv()

        for step in (1, 2):

            @pl.when(m_takes(sweep, step))
            def _():
                m_copy(sweep, step).wait_recv()

    def incoming(sweep, g):
        lanes = slice(LANES * g, LANES * g + LANES)
        far = a_r[sweep, 2, :, lanes]
        mid = a_r[sweep, 1, :, lanes].astype(F32) + by_block(
            FT, [(b, nn(m_r[sweep, 1, 4 * g + b], far)) for b in range(4)]
        )
        mid = mid.astype(BF16)
        return a_r[sweep, 0, :, lanes].astype(F32) + by_block(
            FT, [(b, nn(m_r[sweep, 0, 4 * g + b], mid)) for b in range(4)]
        )

    def corrected(sweep, c, b, entering):
        t = spread(b, entering)
        return m_v[c] - by_block(NU, [(p, nn(e_v[sweep, c, p], t)) for p in range(NP)])

    for copy in halo(0):
        copy.wait_recv()

    @pl.when(s < 3)
    def _():
        up_copy.wait_recv()

    for g in range(2):
        total = jnp.zeros((FT, LANES), F32)
        for b in range(4):
            c = 4 * g + b
            edge = up_r[:, LANES * g : LANES * g + LANES].astype(F32)
            edge = pltpu.roll(edge, (R * (3 - b)) % LANES, 1) if b != 3 else edge
            upper = jnp.where(blocks(FT) == 3, edge, us_v[c]).astype(BF16)
            total = packed(0, c, b, local_sweep(0, c, w_v[c], upper), total)
        a_s[0, :, LANES * g : LANES * g + LANES] = total.astype(BF16)
    send_ends(0)
    take_ends(0)
    for g in range(2):
        entering = incoming(0, g)
        for b in range(4):
            c = 4 * g + b
            middle = corrected(0, c, b, entering)
            picked = nn(sel[0 : 4 * FT], middle.astype(BF16)).astype(BF16)
            ext_l[1][CC + c] = picked[0 : 2 * FT]
            ext_r[1][c] = picked[2 * FT : 4 * FT]
            w_v[c] = middle + x_v[c]
    for copy in halo(1):
        copy.start()
    sections(1)

    for copy in halo(1):
        copy.wait_recv()
    nothing = jnp.zeros((FT, LANES), BF16)
    for g in range(2):
        total = jnp.zeros((FT, LANES), F32)
        for b in range(4):
            c = 4 * g + b
            total = packed(1, c, b, local_sweep(1, c, w_v[c], nothing), total)
        a_s[1, :, LANES * g : LANES * g + LANES] = total.astype(BF16)
    send_ends(1)
    take_ends(1)
    same = (
        lax.broadcasted_iota(jnp.int32, (LANES, LANES), 0)
        == lax.broadcasted_iota(jnp.int32, (LANES, LANES), 1)
    ).astype(BF16)

    def out_store(c):
        return pltpu.make_async_copy(out_v.at[:, c], out_hbm.at[:, c], out_sem.at[c])

    for g in range(2):
        entering = incoming(1, g)
        for b in range(4):
            c = 4 * g + b
            result = corrected(1, c, b, entering).astype(BF16)
            out_v[:, c] = nt(same, result).astype(BF16).reshape(NP, R, NU)
            out_store(c).start()
    for c in range(CC):
        out_store(c).wait()

    for sweep in (0, 1):
        for copy in halo(sweep):
            copy.wait_send()
        for step in (1, 2, 3):

            @pl.when(a_sends(sweep, step))
            def _():
                a_copy(sweep, step).wait_send()

        for step in (1, 2):

            @pl.when(m_sends(sweep, step))
            def _():
                m_copy(sweep, step).wait_send()

    @pl.when(s > 0)
    def _():
        up_copy.wait_send()


def local(crosses, right_sides, initial, inverse_blocks, couplings, neighbours):
    anywhere = pl.BlockSpec(memory_space=pl.ANY)
    vmem = pltpu.VMEM
    dma = pltpu.SemaphoreType.DMA
    return pl.pallas_call(
        functools.partial(kernel, crosses),
        out_shape=jax.ShapeDtypeStruct(right_sides.shape, BF16),
        in_specs=[
            pl.BlockSpec(memory_space=pltpu.SMEM),
            pl.BlockSpec(memory_space=pltpu.VMEM),
            anywhere,
            anywhere,
            anywhere,
            anywhere,
        ],
        out_specs=anywhere,
        scratch_shapes=[
            vmem((NP, CC, R, NU), BF16),
            vmem((NP, CC, R, NU), BF16),
            vmem((NP, CC, NU, NU), BF16),
            vmem((NP, CC, 6, NT, NU), BF16),
            vmem((NP, CC, R, NU), BF16),
            vmem((NP, LOWER + FT, NU), BF16),
            vmem((NP, CC, NU, LOWER + FT), BF16),
            vmem((CC, NU, LANES), F32),
            vmem((CC, NU, LANES), F32),
            vmem((CC, NU, LANES), F32),
            vmem((CC, NU, LANES), F32),
            vmem((CC, FT, LANES), F32),
            vmem((CC, FT, LANES), F32),
            vmem((2, CC, NP, FT, FT), BF16),
            vmem((2, CC, NP, NU, FT), BF16),
            vmem((2 * CC, 2 * FT, LANES), BF16),
            vmem((2 * CC, 2 * FT, LANES), BF16),
            vmem((2 * CC, 2 * FT, LANES), BF16),
            vmem((2 * CC, 2 * FT, LANES), BF16),
            vmem((FT, CC * R), BF16),
            vmem((FT, CC * R), BF16),
            vmem((2, FT, CC * R), BF16),
            vmem((2, 3, FT, CC * R), BF16),
            vmem((2, CC, FT, FT), BF16),
            vmem((2, 2, CC, FT, FT), BF16),
            dma((2,)),
            dma((2, CC)),
            dma((CC,)),
            dma((2, 2)),
            dma((2, 2)),
            dma((2,)),
            dma((2, 3)),
            dma((2, 3)),
            dma((2, 2)),
            dma((2, 2)),
        ],
        compiler_params=pltpu.CompilerParams(
            collective_id=0, has_side_effects=True, vmem_limit_bytes=50 * 1024 * 1024
        ),
        name="sweeps",
    )(
        neighbours,
        jnp.asarray(selector(), BF16),
        right_sides,
        initial,
        inverse_blocks,
        couplings,
    )


def solution(mesh):
    return jax.shard_map(
        functools.partial(local, mesh.shape["cross"]),
        mesh=mesh,
        in_specs=(
            P("sweep", "cross", None, None),
            P("sweep", "cross", None, None),
            P("sweep", "cross", None, None),
            P("sweep", "cross", None, None, None),
            P("cross", None),
        ),
        out_specs=P("sweep", "cross", None, None),
        check_vma=False,
    )
```

time: 234 us -> 68.1 us (0.29)
  matrix products: 121 us -> 0 us
  Pallas kernels: 0 us -> 60.3 us
  starting transfers between devices: 41.8 us -> 0 us
  waiting for transfers between devices: 30.9 us -> 0 us
  local copies, waits for them, and re-layouts: 31.1 us -> 7.72 us
  other arithmetic: 7.65 us -> 0 us
    dot_general x75 -> x0, matrix products: 121 us -> none  [the longest x33 55.6 us: face_trace(): jnp.dot(field, selector(axis_place, which), preferred_element_type=jnp.fl...]
    pallas_call x0 -> x1, Pallas kernels: none -> 60.3 us  [local(): pl.pallas_call(functools.partial(kernel, crosses), out_shape=jax.ShapeDty...]
    ppermute x11 -> x0, starting transfers between devices: 41.8 us -> none  [the longest x7 19.8 us: passed_along(): return lax.ppermute(block, axis, route)]
    ppermute x11 -> x0, waiting for transfers between devices: 30.9 us -> none  [the longest x7 16 us: passed_along(): return lax.ppermute(block, axis, route)]
    gather x8 -> x0, local copies, waits for them, and re-layouts: 16.7 us -> none  [cross_terms(): picked = jnp.take(extended, lower_which[:, face], axis=1)]
    slice x2 -> x0, local copies, waits for them, and re-layouts: 6.69 us -> none  [the longest x1 3.66 us: local(): couplings[:, :, 0]]
    unnamed x66 -> x12, local copies, waits for them, and re-layouts: 2.91 us -> 7.72 us
    select_n x3 -> x0, other arithmetic: 4.42 us -> none  [the longest x2 4.41 us: cross_terms(): picked = jnp.take(extended, lower_which[:, face], axis=1)]
  transfers between devices with their start and end apart: 11 -> 0, of which waited for: 8 -> 0; matrix products, arithmetic and copies ran while one was open for 19% -> 0% of each run, Pallas kernels for 0% -> 0%
where the time goes in v1:
time: 68.1 us; the launch traced here: 68 us
  Pallas kernels  60.3 us (89%)
  local copies, waits for them, and re-layouts  7.72 us (11%)
    pallas_call x1, Pallas kernels, local(): pl.pallas_call(functools.partial(kernel, crosses), out_shape=jax.ShapeDty...  60.3 us
    unnamed x12, local copies, waits for them, and re-layouts  7.72 us

profile of v1, /device:TPU:1, one launch (start us, length us, event | category | flops | bytes accessed | tf_op | source)
XLA Modules:
  0.0 68.0 jit_solution(14656744965591075290)
XLA Ops:
  0.0 0.8 %copy.7.neigh = s32[8,4]{1,0:T(8,128)S(1)} copy(s32[8,4]{0,1:T(4,128)} %param.10) | data formatting | bytes 256 | tf_op args[4]
  0.8 0.0 copy-start.3
  0.8 2.2 %copy.8.inv_hbm = bf16[4,8,135,135]{3,2,1,0:T(8,128)(2,1)S(1)} copy(bf16[4,8,135,135]{3,1,2,0:T(8,128)(2,1)} %param.8) | data formatting | bytes 2332800 | tf_op args[2]
  3.0 0.7 %copy-done.3 = bf16[4,8,6,45,135]{4,1,3,2,0:T(8,128)(2,1)S(1)} copy-done((bf16[4,8,6,45,135]{4,1,3,2,0:T(8,128)(2,1)S(1)}, bf16[4,8,6,45,135]{4,1,3,2,0:T(8,128)(2,1)}, u32[]{:S(2)}) %copy-start.3) | copy-done | bytes 2332824
  3.7 0.0 copy-start
  3.7 0.0 copy-start.1
  3.7 0.0 copy-start.2
  3.7 3.2 %copy.9.cpl_hbm = bf16[4,8,6,45,135]{4,3,2,1,0:T(8,128)(2,1)} copy(bf16[4,8,6,45,135]{4,1,3,2,0:T(8,128)(2,1)S(1)} %copy-done.3) | data formatting | bytes 4665600 | tf_op args[3]
  6.9 0.0 copy-done
  6.9 0.0 copy-done.1
  6.9 0.0 copy-done.2
  6.9 60.3 %sweeps.1 = bf16[4,8,32,135]{3,2,1,0:T(8,128)(2,1)S(1)} custom-call(s32[8,4]{1,0:T(8,128)S(1)} %copy.7.neigh, bf16[288,135]{1,0:T(8,128)(2,1)S(1)} %copy-done.2, bf16[4,8,32,135]{3,2,1,0:T(8,128)(2,1)S(1)} %copy-done, bf16[4,8,32,135]{3,2,1,0:T(8,128)(2,1)S(1)} %copy-done.1, bf16[4,8,135,135]{3,2,1,0:T(8,128)(2,1)S(1)} %copy.8.inv_hbm, ...), custom_call_target="tpu_custom_call" | custom-call | tf_op jit(solution)/shard_map/sweeps/pallas_call | solution.py:461
  67.2 0.8 %copy.11 = bf16[4,8,32,135]{3,2,1,0:T(8,128)(2,1)} copy(bf16[4,8,32,135]{3,2,1,0:T(8,128)(2,1)S(1)} %sweeps.1) | data formatting | bytes 552960
Async XLA Ops:
  0.8 2.9 %copy-start.3 = (bf16[4,8,6,45,135]{4,1,3,2,0:T(8,128)(2,1)S(1)}, bf16[4,8,6,45,135]{4,1,3,2,0:T(8,128)(2,1)}, u32[]{:S(2)}) copy-start(bf16[4,8,6,45,135]{4,1,3,2,0:T(8,128)(2,1)} %param.9) | copy-start | bytes 6998404
  3.7 3.2 %copy-start = (bf16[4,8,32,135]{3,2,1,0:T(8,128)(2,1)S(1)}, bf16[4,8,32,135]{3,2,1,0:T(8,128)(2,1)}, u32[]{:S(2)}) copy-start(bf16[4,8,32,135]{3,2,1,0:T(8,128)(2,1)} %rhs_hbm.1) | copy-start | bytes 829444
  3.7 3.3 %copy-start.1 = (bf16[4,8,32,135]{3,2,1,0:T(8,128)(2,1)S(1)}, bf16[4,8,32,135]{3,2,1,0:T(8,128)(2,1)}, u32[]{:S(2)}) copy-start(bf16[4,8,32,135]{3,2,1,0:T(8,128)(2,1)} %init_hbm.1) | copy-start | bytes 829444
  3.7 3.3 %copy-start.2 = (bf16[288,135]{1,0:T(8,128)(2,1)S(1)}, bf16[288,135]{1,0:T(8,128)(2,1)}, u32[]{:S(2)}) copy-start(bf16[288,135]{1,0:T(8,128)(2,1)} %constant.2.clone.sel) | copy-start | bytes 233284

commit v2 on v1

v2 whole, which is shorter than its diff:
```python
import functools

import jax
import jax.numpy as jnp
import numpy as np
from jax import lax
from jax.experimental import pallas as pl
from jax.experimental.pallas import tpu as pltpu
from jax.sharding import PartitionSpec as P

MESH = pl.DeviceIdType.MESH
NU, NT, R, CC, NP = 135, 45, 32, 8, 4
FT = 48
LANES = NP * R
NUP = 144
F32, BF16 = jnp.float32, jnp.bfloat16
FACES = ((1, 2), (2, 2), (1, 0), (2, 0), (0, 0), (0, 2))
STACK = (1, 2, 3, 4, 5)
NSTACK = len(STACK) * FT
LOWER = 256


def selector():
    rows = np.zeros((len(FACES) * FT, NU), np.float32)
    for face, (axis_place, which) in enumerate(FACES):
        for slot in range(NT):
            v, first, second = slot // 9, slot // 3 % 3, slot % 3
            node = [first, second]
            node.insert(axis_place, which)
            rows[face * FT + slot, v * 27 + node[0] * 9 + node[1] * 3 + node[2]] = 1.0
    return rows


def nn(a, b):
    return lax.dot_general(a, b, (((1,), (0,)), ((), ())), preferred_element_type=F32)


def nt(a, b):
    return lax.dot_general(a, b, (((1,), (1,)), ((), ())), preferred_element_type=F32)


def blocks(rows):
    return lax.broadcasted_iota(jnp.int32, (rows, LANES), 1) // R


def by_block(rows, parts):
    block = blocks(rows)
    total = parts[0][1]
    for b, part in parts[1:]:
        total = jnp.where(block == b, part, total)
    return total


def kernel(
    crosses,
    neigh,
    sel,
    rhs_hbm,
    init_hbm,
    inv_hbm,
    cpl_hbm,
    out_v,
    init_v,
    rhs_v,
    inv_n,
    cpl_n,
    turn_v,
    inv_v,
    stack_v,
    d_v,
    rows_v,
    w_v,
    x_v,
    v_v,
    t_v,
    us_v,
    q_v,
    l1_v,
    l2_v,
    l3_v,
    li_v,
    ext_l0,
    ext_l1,
    ext_r0,
    ext_r1,
    up_s,
    up_r,
    a_s,
    a_r,
    m_s,
    m_r,
    load_sem,
    plane_sem,
    halo_s,
    halo_r,
    upsem,
    a_ss,
    a_rs,
    m_ss,
    m_rs,
):
    ext_l, ext_r = (ext_l0, ext_l1), (ext_r0, ext_r1)
    s = lax.axis_index("sweep")
    k = lax.axis_index("cross")
    right = lax.rem(k + 1, crosses)
    left = lax.rem(k + crosses - 1, crosses)

    load_init = pltpu.make_async_copy(init_hbm, init_v, load_sem.at[0])
    load_rhs = pltpu.make_async_copy(rhs_hbm, rhs_v, load_sem.at[1])

    def inv_load(p):
        return pltpu.make_async_copy(inv_hbm.at[p], inv_n.at[p], plane_sem.at[0, p])

    def cpl_load(p):
        return pltpu.make_async_copy(cpl_hbm.at[p], cpl_n.at[p], plane_sem.at[1, p])

    load_init.start()
    for p in range(NP):
        inv_load(p).start()
        cpl_load(p).start()
    load_rhs.start()

    barrier = pltpu.get_barrier_semaphore()
    for other in (left, right):
        pl.semaphore_signal(barrier, inc=1, device_id={"cross": other}, device_id_type=MESH)
    for step in (1, 2, 3):
        pl.semaphore_signal(
            barrier, inc=1, device_id={"sweep": lax.rem(s + step, 4)}, device_id_type=MESH
        )

    load_init.wait()
    up_s[...] = nt(sel[4 * FT : 5 * FT], init_v[0].reshape(CC * R, NU)).astype(BF16)
    for c in range(CC):
        picked = nt(sel[0 : 5 * FT], init_v[:, c].reshape(LANES, NU))
        ext_l[0][CC + c] = picked[0 : 2 * FT].astype(BF16)
        ext_r[0][c] = picked[2 * FT : 4 * FT].astype(BF16)
        us_v[c] = pltpu.roll(picked[4 * FT : 5 * FT], LANES - R, 1)
    pl.semaphore_wait(barrier, 5)

    def halo(sweep):
        return (
            pltpu.make_async_remote_copy(
                ext_l[sweep].at[pl.ds(CC, CC)],
                ext_l[sweep].at[pl.ds(0, CC)],
                halo_s.at[sweep, 0],
                halo_r.at[sweep, 0],
                device_id={"cross": right},
                device_id_type=MESH,
            ),
            pltpu.make_async_remote_copy(
                ext_r[sweep].at[pl.ds(0, CC)],
                ext_r[sweep].at[pl.ds(CC, CC)],
                halo_s.at[sweep, 1],
                halo_r.at[sweep, 1],
                device_id={"cross": left},
                device_id_type=MESH,
            ),
        )

    up_copy = pltpu.make_async_remote_copy(
        up_s,
        up_r,
        upsem.at[0],
        upsem.at[1],
        device_id={"sweep": lax.rem(s + 3, 4)},
        device_id_type=MESH,
    )
    for copy in halo(0):
        copy.start()

    @pl.when(s > 0)
    def _():
        up_copy.start()

    def a_copy(sweep, step):
        to = lax.rem(s + step, 4) if sweep == 0 else lax.rem(s + 4 - step, 4)
        return pltpu.make_async_remote_copy(
            a_s.at[sweep],
            a_r.at[sweep, step - 1],
            a_ss.at[sweep, step - 1],
            a_rs.at[sweep, step - 1],
            device_id={"sweep": to},
            device_id_type=MESH,
        )

    def m_copy(sweep, step):
        to = lax.rem(s + step, 4) if sweep == 0 else lax.rem(s + 4 - step, 4)
        return pltpu.make_async_remote_copy(
            m_s.at[sweep],
            m_r.at[sweep, step - 1],
            m_ss.at[sweep, step - 1],
            m_rs.at[sweep, step - 1],
            device_id={"sweep": to},
            device_id_type=MESH,
        )

    def a_sends(sweep, step):
        return s + step < 4 if sweep == 0 else s >= step

    def a_takes(sweep, step):
        return s >= step if sweep == 0 else s + step < 4

    def m_sends(sweep, step):
        if sweep == 0:
            return jnp.logical_and(s >= 1, s + step < 4)
        return jnp.logical_and(s <= 2, s >= step)

    def m_takes(sweep, step):
        return s >= step + 1 if sweep == 0 else s + step <= 2

    @pl.when(s == 3)
    def _():
        up_r[...] = jnp.zeros_like(up_r)

    for step in (1, 2, 3):

        @pl.when(s < step)
        def _():
            a_r[0, step - 1] = jnp.zeros((FT, CC * R), BF16)

        @pl.when(s + step > 3)
        def _():
            a_r[1, step - 1] = jnp.zeros((FT, CC * R), BF16)

    for step in (1, 2):

        @pl.when(s < step + 1)
        def _():
            m_r[0, step - 1] = jnp.zeros((CC, FT, FT), BF16)

        @pl.when(s + step > 2)
        def _():
            m_r[1, step - 1] = jnp.zeros((CC, FT, FT), BF16)

    inv_v[:, :, NU - 7 : NUP] = jnp.zeros((CC, NP, NUP - NU + 7, NU), BF16)
    for place in list(range(len(STACK))) + [LOWER // FT]:
        top = LOWER if place == LOWER // FT else FT * place
        stack_v[:, :, top + 32 : top + FT] = jnp.zeros((CC, NP, 16, NU), BF16)
    stack_v[:, :, NSTACK:LOWER] = jnp.zeros((CC, NP, LOWER - NSTACK, NU), BF16)
    q_v[...] = jnp.zeros_like(q_v)

    def turn(slot, block, count, to, p, first):
        flat = block.astype(F32).reshape(CC * count, NU)
        turn_v[0, slot, 0 : CC * count] = flat[:, 0:128]
        turn_v[1, slot, 0 : CC * count, 0 : NU - 128] = flat[:, 128:NU]
        for c in range(CC):
            rows = pl.ds(c, count, stride=CC)
            to[c, p, first : first + count, 0:128] = turn_v[0, slot, rows].astype(BF16)
            to[c, p, first : first + count, 128:NU] = turn_v[1, slot, rows][
                :, 0 : NU - 128
            ].astype(BF16)

    def products(p, carry):
        inv_load(p).wait()
        cpl_load(p).wait()
        slot = 0
        for first in range(0, NU, 16):
            count = min(16, NU - first)
            turn(slot, inv_n[p, first : first + count], count, inv_v, p, first)
            slot += 1
        for top, face in [(FT * place, face) for place, face in enumerate(STACK)] + [(LOWER, 0)]:
            for first in range(0, NT, 16):
                count = min(16, NT - first)
                block = cpl_n[p, face, first : first + count]
                turn(slot, block, count, stack_v, p, top + first)
                slot += 1
        for c in range(CC):
            d = nt(inv_v[c, p], stack_v[c, p])
            d_v[c, p] = d.astype(BF16)
            rows_v[0, c] = d[:, LOWER : LOWER + FT]
            rows_v[1, c] = d[:, 0:FT]
            for var in range(5):
                to = slice(9 * var, 9 * var + 9)
                q_v[0, c, p, to] = rows_v[0, c, 27 * var + 18 : 27 * var + 27]
                q_v[1, c, p, to] = rows_v[1, c, 27 * var : 27 * var + 9]
        return carry

    lax.fori_loop(0, NP, products, 0)
    load_rhs.wait()

    def by_plane(rows, stacked):
        return by_block(rows, [(p, stacked[rows * p : rows * p + rows]) for p in range(NP)])

    for c in range(CC):
        rhs = rhs_v[:, c].reshape(LANES, NU)
        w_v[c] = by_plane(NUP, nt(inv_v[c].reshape(NP * NUP, NU), rhs))

    def order_of(sweep):
        return list(range(NP)) if sweep == 0 else list(range(NP - 1, -1, -1))

    def sections(sweep):
        order = order_of(sweep)
        n = [[(-q_v[sweep, c, p]).astype(BF16) for p in order] for c in range(CC)]
        two = [
            [nn(n[c][o], n[c][o - 1]).astype(BF16) for o in (1, 2, 3)] for c in range(CC)
        ]
        for c in range(CC):
            for o in (1, 2, 3):
                l1_v[sweep, c, FT * (o - 1) : FT * o] = n[c][o]
            for o in (2, 3):
                l2_v[sweep, c, FT * (o - 2) : FT * (o - 1)] = two[c][o - 1]
            li_v[sweep, c, 0:FT] = n[c][0]
            li_v[sweep, c, FT : 2 * FT] = two[c][0]
            li_v[sweep, c, 2 * FT : 3 * FT] = nn(two[c][1], n[c][0]).astype(BF16)
            l3_v[sweep, c] = nn(two[c][2], n[c][1]).astype(BF16)
            m_s[sweep, c] = nn(two[c][2], two[c][0]).astype(BF16)
        for step in (1, 2):

            @pl.when(m_sends(sweep, step))
            def _():
                m_copy(sweep, step).start()

    sections(0)

    def gathered(sweep, c, upper):
        low = lax.rem(neigh[2, c] - (k - 1) * CC + 2 * crosses * CC, crosses * CC)
        high = lax.rem(neigh[3, c] - k * CC + crosses * CC, crosses * CC)
        low = jnp.clip(low, 0, 2 * CC - 1)
        high = jnp.clip(high, 0, 2 * CC - 1)
        return jnp.concatenate(
            [
                upper,
                ext_l[sweep][c, 0:FT],
                ext_r[sweep][CC + c, 0:FT],
                ext_l[sweep][low, FT : 2 * FT],
                ext_r[sweep][high, FT : 2 * FT],
            ],
            axis=0,
        )

    def shift_of(sweep, steps):
        return R * steps if sweep == 0 else LANES - R * steps

    def local_sweep(sweep, c, base, upper):
        order = order_of(sweep)
        stack = gathered(sweep, c, upper)
        x = by_plane(NUP, nn(d_v[c].reshape(NP * NUP, LOWER + FT)[:, 0:NSTACK], stack))
        v = base - x
        v_v[c] = v
        if sweep == 0:
            x_v[c] = x
        start = 18 if sweep == 0 else 0
        pieces = [v_v[c, 27 * var + start : 27 * var + start + 9] for var in range(5)]
        for var in range(5):
            t_v[c, 9 * var : 9 * var + 9] = pieces[var]
        u = t_v[c]
        block = blocks(FT)
        total = u
        for steps, left_v in ((1, l1_v), (2, l2_v), (3, l3_v)):
            moved = pltpu.roll(u, shift_of(sweep, steps), 1).astype(BF16)
            z = nn(left_v[sweep, c], moved)
            for o in range(steps, NP):
                part = z[FT * (o - steps) : FT * (o - steps + 1)]
                total = total + jnp.where(block == order[o], part, 0.0)
        return total

    def packed(sweep, b, now, total):
        last = 3 if sweep == 0 else 0
        turned_in = now if b == last else pltpu.roll(now, (R * (b - last)) % LANES, 1)
        return jnp.where(blocks(FT) == b, turned_in, total)

    def spread(b, group):
        one = jnp.where(blocks(FT) == b, group, 0.0)
        one = one + pltpu.roll(one, R, 1)
        return one + pltpu.roll(one, 2 * R, 1)

    def send_ends(sweep):
        for step in (1, 2, 3):

            @pl.when(a_sends(sweep, step))
            def _():
                a_copy(sweep, step).start()

    def take_ends(sweep):
        for step in (1, 2, 3):

            @pl.when(a_takes(sweep, step))
            def _():
                a_copy(sweep, step).wait_recv()

        for step in (1, 2):

            @pl.when(m_takes(sweep, step))
            def _():
                m_copy(sweep, step).wait_recv()

    def incoming(sweep, g):
        lanes = slice(LANES * g, LANES * g + LANES)

        def applied(step, ends):
            return by_block(FT, [(b, nn(m_r[sweep, step, 4 * g + b], ends)) for b in range(4)])

        mid = a_r[sweep, 1, :, lanes].astype(F32) + applied(1, a_r[sweep, 2, :, lanes])
        return a_r[sweep, 0, :, lanes].astype(F32) + applied(0, mid.astype(BF16))

    def corrected(sweep, c, b, entering):
        order = order_of(sweep)
        t = spread(b, entering)
        z = nn(li_v[sweep, c], t.astype(BF16))
        before = by_block(
            FT, [(order[0], t)] + [(order[o], z[FT * (o - 1) : FT * o]) for o in (1, 2, 3)]
        )
        local_part = pltpu.roll(t_v[c], shift_of(sweep, 1), 1)
        before = before + jnp.where(blocks(FT) == order[0], 0.0, local_part)
        low = LOWER if sweep == 0 else 0
        d = d_v[c].reshape(NP * NUP, LOWER + FT)[:, low : low + FT]
        return v_v[c] - by_plane(NUP, nn(d, before.astype(BF16)))

    for copy in halo(0):
        copy.wait_recv()

    @pl.when(s < 3)
    def _():
        up_copy.wait_recv()

    t_v[...] = jnp.zeros_like(t_v)
    for g in range(2):
        total = jnp.zeros((FT, LANES), F32)
        for b in range(4):
            c = 4 * g + b
            edge = up_r[:, LANES * g : LANES * g + LANES].astype(F32)
            edge = pltpu.roll(edge, (R * (3 - b)) % LANES, 1) if b != 3 else edge
            upper = jnp.where(blocks(FT) == 3, edge, us_v[c]).astype(BF16)
            now = local_sweep(0, c, w_v[c], upper)
            t_v[c] = now
            total = packed(0, b, now, total)
        a_s[0, :, LANES * g : LANES * g + LANES] = total.astype(BF16)
    send_ends(0)
    take_ends(0)
    for g in range(2):
        entering = incoming(0, g)
        for b in range(4):
            c = 4 * g + b
            middle = corrected(0, c, b, entering)
            picked = nn(sel[0 : 4 * FT], middle[0:NU].astype(BF16)).astype(BF16)
            ext_l[1][CC + c] = picked[0 : 2 * FT]
            ext_r[1][c] = picked[2 * FT : 4 * FT]
            w_v[c] = middle + x_v[c]
    for copy in halo(1):
        copy.start()
    sections(1)

    for copy in halo(1):
        copy.wait_recv()
    nothing = jnp.zeros((FT, LANES), BF16)
    for g in range(2):
        total = jnp.zeros((FT, LANES), F32)
        for b in range(4):
            c = 4 * g + b
            now = local_sweep(1, c, w_v[c], nothing)
            t_v[c] = now
            total = packed(1, b, now, total)
        a_s[1, :, LANES * g : LANES * g + LANES] = total.astype(BF16)
    send_ends(1)
    take_ends(1)
    same = (
        lax.broadcasted_iota(jnp.int32, (LANES, LANES), 0)
        == lax.broadcasted_iota(jnp.int32, (LANES, LANES), 1)
    ).astype(BF16)
    for g in range(2):
        entering = incoming(1, g)
        for b in range(4):
            c = 4 * g + b
            result = corrected(1, c, b, entering)[0:NU].astype(BF16)
            out_v[:, c] = nt(same, result).astype(BF16).reshape(NP, R, NU)

    for sweep in (0, 1):
        for copy in halo(sweep):
            copy.wait_send()
        for step in (1, 2, 3):

            @pl.when(a_sends(sweep, step))
            def _():
                a_copy(sweep, step).wait_send()

        for step in (1, 2):

            @pl.when(m_sends(sweep, step))
            def _():
                m_copy(sweep, step).wait_send()

    @pl.when(s > 0)
    def _():
        up_copy.wait_send()


def local(crosses, right_sides, initial, inverse_blocks, couplings, neighbours):
    hbm = pl.BlockSpec(memory_space=pltpu.HBM)
    vmem = pltpu.VMEM
    dma = pltpu.SemaphoreType.DMA
    return pl.pallas_call(
        functools.partial(kernel, crosses),
        out_shape=jax.ShapeDtypeStruct(right_sides.shape, BF16),
        in_specs=[
            pl.BlockSpec(memory_space=pltpu.SMEM),
            pl.BlockSpec(memory_space=pltpu.VMEM),
            hbm,
            hbm,
            hbm,
            hbm,
        ],
        out_specs=pl.BlockSpec(memory_space=pltpu.VMEM),
        scratch_shapes=[
            vmem((NP, CC, R, NU), BF16),
            vmem((NP, CC, R, NU), BF16),
            vmem((NP, NU, CC, NU), BF16),
            vmem((NP, 6, NT, CC, NU), BF16),
            vmem((2, 27, 16 * CC, 128), F32),
            vmem((CC, NP, NUP, NU), BF16),
            vmem((CC, NP, LOWER + FT, NU), BF16),
            vmem((CC, NP, NUP, LOWER + FT), BF16),
            vmem((2, CC, NUP, FT), F32),
            vmem((CC, NUP, LANES), F32),
            vmem((CC, NUP, LANES), F32),
            vmem((CC, NUP, LANES), F32),
            vmem((CC, FT, LANES), F32),
            vmem((CC, FT, LANES), F32),
            vmem((2, CC, NP, FT, FT), F32),
            vmem((2, CC, 3 * FT, FT), BF16),
            vmem((2, CC, 2 * FT, FT), BF16),
            vmem((2, CC, FT, FT), BF16),
            vmem((2, CC, 3 * FT, FT), BF16),
            vmem((2 * CC, 2 * FT, LANES), BF16),
            vmem((2 * CC, 2 * FT, LANES), BF16),
            vmem((2 * CC, 2 * FT, LANES), BF16),
            vmem((2 * CC, 2 * FT, LANES), BF16),
            vmem((FT, CC * R), BF16),
            vmem((FT, CC * R), BF16),
            vmem((2, FT, CC * R), BF16),
            vmem((2, 3, FT, CC * R), BF16),
            vmem((2, CC, FT, FT), BF16),
            vmem((2, 2, CC, FT, FT), BF16),
            dma((2,)),
            dma((2, NP)),
            dma((2, 2)),
            dma((2, 2)),
            dma((2,)),
            dma((2, 3)),
            dma((2, 3)),
            dma((2, 2)),
            dma((2, 2)),
        ],
        compiler_params=pltpu.CompilerParams(
            collective_id=0, has_side_effects=True, vmem_limit_bytes=56 * 1024 * 1024
        ),
        name="sweeps",
    )(
        neighbours.T,
        jnp.asarray(selector(), BF16),
        right_sides,
        initial,
        inverse_blocks.transpose(0, 2, 1, 3),
        couplings.transpose(0, 2, 3, 1, 4),
    )


def solution(mesh):
    return jax.shard_map(
        functools.partial(local, mesh.shape["cross"]),
        mesh=mesh,
        in_specs=(
            P("sweep", "cross", None, None),
            P("sweep", "cross", None, None),
            P("sweep", "cross", None, None),
            P("sweep", "cross", None, None, None),
            P("cross", None),
        ),
        out_specs=P("sweep", "cross", None, None),
        check_vma=False,
    )
```

time: 68.1 us -> 53.2 us (0.78)
  Pallas kernels: 60.3 us -> 51.2 us
  local copies, waits for them, and re-layouts: 7.72 us -> 1.87 us
    pallas_call x1, Pallas kernels: 60.3 us -> 51.2 us  [local(): pl.pallas_call(functools.partial(kernel, crosses), out_shape=jax.ShapeDty...]
    unnamed x12 -> x1, local copies, waits for them, and re-layouts: 7.72 us -> 1.87 us
where the time goes in v2:
time: 53.2 us; the launch traced here: 53.1 us
  Pallas kernels  51.2 us (96%)
  local copies, waits for them, and re-layouts  1.87 us (4%)
    pallas_call x1, Pallas kernels, local(): pl.pallas_call(functools.partial(kernel, crosses), out_shape=jax.ShapeDty...  51.2 us
    unnamed x1, local copies, waits for them, and re-layouts  1.87 us

profile of v2, /device:TPU:1, one launch (start us, length us, event | category | flops | bytes accessed | tf_op | source)
XLA Modules:
  0.0 53.1 jit_solution(9421519823166366125)
XLA Ops:
  0.0 51.2 %sweeps.1 = bf16[4,8,32,135]{3,2,1,0:T(8,128)(2,1)} custom-call(s32[4,8]{1,0:T(4,128)} %bitcast.5, bf16[288,135]{1,0:T(8,128)(2,1)} %constant.2.clone.sel, bf16[4,8,32,135]{3,2,1,0:T(8,128)(2,1)} %rhs_hbm.1, bf16[4,8,32,135]{3,2,1,0:T(8,128)(2,1)} %init_hbm.1, bf16[4,135,8,135]{3,2,1,0:T(8,128)(2,1)} %bitcast.4, bf16[4,6,45,8,135]{4,3,2,1,0:T(8,128)(2,1)} %bitcast.3), custom_call_target="tpu_custom_call" | custom-call | tf_op jit(solution)/shard_map/sweeps/pallas_call | solution.py:491
  51.2 1.9 %copy.8 = bf16[4,8,32,135]{3,2,1,0:T(8,128)(2,1)} copy(bf16[4,8,32,135]{3,2,1,0:T(8,128)(2,1)} %sweeps.1) | data formatting | bytes 552960

commit v3 on v2

--- a/solution.py
+++ b/solution.py
@@ -14,20 +14,29 @@
 LANES = NP * R
 NUP = 144
 F32, BF16 = jnp.float32, jnp.bfloat16
-FACES = ((1, 2), (2, 2), (1, 0), (2, 0), (0, 0), (0, 2))
+WT = 80
 STACK = (1, 2, 3, 4, 5)
 NSTACK = len(STACK) * FT
 LOWER = 256
+CHUNK = 2
 
 
 def selector():
-    rows = np.zeros((len(FACES) * FT, NU), np.float32)
-    for face, (axis_place, which) in enumerate(FACES):
-        for slot in range(NT):
-            v, first, second = slot // 9, slot // 3 % 3, slot % 3
-            node = [first, second]
-            node.insert(axis_place, which)
-            rows[face * FT + slot, v * 27 + node[0] * 9 + node[1] * 3 + node[2]] = 1.0
+    rows = np.zeros((2 * WT + 3 * FT, NU), np.float32)
+    for half, which in enumerate((2, 0)):
+        others = [node for node in range(3) if node != which]
+        for v in range(5):
+            for a in range(3):
+                for b in range(3):
+                    rows[half * WT + 9 * v + 3 * a + b, 27 * v + 9 * a + 3 * b + which] = 1.0
+                for place, c in enumerate(others):
+                    slot = NT + 6 * v + 2 * a + place
+                    rows[half * WT + slot, 27 * v + 9 * a + 3 * which + c] = 1.0
+                    rows[2 * WT + FT * (1 + half) + 9 * v + 3 * a + c, slot] = 1.0
+                slot = 9 * v + 3 * a + which
+                rows[2 * WT + FT * (1 + half) + slot, slot] = 1.0
+    for v in range(5):
+        rows[2 * WT + 9 * v : 2 * WT + 9 * v + 9, 27 * v : 27 * v + 9] = np.eye(9)
     return rows
 
 
@@ -53,15 +62,18 @@
 
 def kernel(
     crosses,
-    neigh,
-    sel,
+    neigh_hbm,
+    sel_hbm,
     rhs_hbm,
     init_hbm,
     inv_hbm,
     cpl_hbm,
-    out_v,
+    out_hbm,
+    neigh,
+    sel,
     init_v,
     rhs_v,
+    out_v,
     inv_n,
     cpl_n,
     turn_v,
@@ -78,7 +90,8 @@
     l1_v,
     l2_v,
     l3_v,
-    li_v,
+    e_v,
+    mm_v,
     ext_l0,
     ext_l1,
     ext_r0,
@@ -91,6 +104,7 @@
     m_r,
     load_sem,
     plane_sem,
+    out_sem,
     halo_s,
     halo_r,
     upsem,
@@ -114,11 +128,15 @@
     def cpl_load(p):
         return pltpu.make_async_copy(cpl_hbm.at[p], cpl_n.at[p], plane_sem.at[1, p])
 
+    load_sel = pltpu.make_async_copy(sel_hbm, sel, load_sem.at[2])
+    load_neigh = pltpu.make_async_copy(neigh_hbm, neigh, load_sem.at[3])
+    load_sel.start()
     load_init.start()
     for p in range(NP):
         inv_load(p).start()
         cpl_load(p).start()
     load_rhs.start()
+    load_neigh.start()
 
     barrier = pltpu.get_barrier_semaphore()
     for other in (left, right):
@@ -128,33 +146,20 @@
             barrier, inc=1, device_id={"sweep": lax.rem(s + step, 4)}, device_id_type=MESH
         )
 
-    load_init.wait()
-    up_s[...] = nt(sel[4 * FT : 5 * FT], init_v[0].reshape(CC * R, NU)).astype(BF16)
-    for c in range(CC):
-        picked = nt(sel[0 : 5 * FT], init_v[:, c].reshape(LANES, NU))
-        ext_l[0][CC + c] = picked[0 : 2 * FT].astype(BF16)
-        ext_r[0][c] = picked[2 * FT : 4 * FT].astype(BF16)
-        us_v[c] = pltpu.roll(picked[4 * FT : 5 * FT], LANES - R, 1)
-    pl.semaphore_wait(barrier, 5)
-
-    def halo(sweep):
+    def halo(sweep, part):
+        def copy(ext, direction, first, to, other):
+            return pltpu.make_async_remote_copy(
+                ext.at[pl.ds(first + CHUNK * part, CHUNK)],
+                ext.at[pl.ds(to + CHUNK * part, CHUNK)],
+                halo_s.at[sweep, direction, part],
+                halo_r.at[sweep, direction, part],
+                device_id={"cross": other},
+                device_id_type=MESH,
+            )
+
         return (
-            pltpu.make_async_remote_copy(
-                ext_l[sweep].at[pl.ds(CC, CC)],
-                ext_l[sweep].at[pl.ds(0, CC)],
-                halo_s.at[sweep, 0],
-                halo_r.at[sweep, 0],
-                device_id={"cross": right},
-                device_id_type=MESH,
-            ),
-            pltpu.make_async_remote_copy(
-                ext_r[sweep].at[pl.ds(0, CC)],
-                ext_r[sweep].at[pl.ds(CC, CC)],
-                halo_s.at[sweep, 1],
-                halo_r.at[sweep, 1],
-                device_id={"cross": left},
-                device_id_type=MESH,
-            ),
+            copy(ext_l[sweep], 0, CC, 0, right),
+            copy(ext_r[sweep], 1, 0, CC, left),
         )
 
     up_copy = pltpu.make_async_remote_copy(
@@ -165,8 +170,20 @@
         device_id={"sweep": lax.rem(s + 3, 4)},
         device_id_type=MESH,
     )
-    for copy in halo(0):
-        copy.start()
+
+    load_sel.wait()
+    load_init.wait()
+    up_s[...] = nt(sel[2 * WT : 2 * WT + FT], init_v[0].reshape(CC * R, NU)).astype(BF16)
+    for c in range(CC):
+        picked = nt(sel[0 : 2 * WT + FT, 0:NU], init_v[:, c].reshape(LANES, NU))
+        ext_l[0][CC + c] = picked[0:WT].astype(BF16)
+        ext_r[0][c] = picked[WT : 2 * WT].astype(BF16)
+        us_v[c] = pltpu.roll(picked[2 * WT : 2 * WT + FT], LANES - R, 1)
+        if c == CHUNK - 1:
+            pl.semaphore_wait(barrier, 5)
+        if c % CHUNK == CHUNK - 1:
+            for copy in halo(0, c // CHUNK):
+                copy.start()
 
     @pl.when(s > 0)
     def _():
@@ -288,6 +305,10 @@
     def order_of(sweep):
         return list(range(NP)) if sweep == 0 else list(range(NP - 1, -1, -1))
 
+    def d_in(sweep, c):
+        low = LOWER if sweep == 0 else 0
+        return d_v[c, :, :, low : low + FT]
+
     def sections(sweep):
         order = order_of(sweep)
         n = [[(-q_v[sweep, c, p]).astype(BF16) for p in order] for c in range(CC)]
@@ -299,9 +320,10 @@
                 l1_v[sweep, c, FT * (o - 1) : FT * o] = n[c][o]
             for o in (2, 3):
                 l2_v[sweep, c, FT * (o - 2) : FT * (o - 1)] = two[c][o - 1]
-            li_v[sweep, c, 0:FT] = n[c][0]
-            li_v[sweep, c, FT : 2 * FT] = two[c][0]
-            li_v[sweep, c, 2 * FT : 3 * FT] = nn(two[c][1], n[c][0]).astype(BF16)
+            e_v[sweep, c, order[0]] = d_in(sweep, c)[order[0]]
+            fronts = (n[c][0], two[c][0], nn(two[c][1], n[c][0]).astype(BF16))
+            for o in (1, 2, 3):
+                e_v[sweep, c, order[o]] = nn(d_in(sweep, c)[order[o]], fronts[o - 1]).astype(BF16)
             l3_v[sweep, c] = nn(two[c][2], n[c][1]).astype(BF16)
             m_s[sweep, c] = nn(two[c][2], two[c][0]).astype(BF16)
         for step in (1, 2):
@@ -317,13 +339,14 @@
         high = lax.rem(neigh[3, c] - k * CC + crosses * CC, crosses * CC)
         low = jnp.clip(low, 0, 2 * CC - 1)
         high = jnp.clip(high, 0, 2 * CC - 1)
+        apart = [sel[2 * WT + FT * half : 2 * WT + FT * half + FT, 0:WT] for half in (1, 2)]
         return jnp.concatenate(
             [
                 upper,
-                ext_l[sweep][c, 0:FT],
-                ext_r[sweep][CC + c, 0:FT],
-                ext_l[sweep][low, FT : 2 * FT],
-                ext_r[sweep][high, FT : 2 * FT],
+                nn(apart[0], ext_l[sweep][c]).astype(BF16),
+                nn(apart[1], ext_r[sweep][CC + c]).astype(BF16),
+                ext_l[sweep][low, 0:FT],
+                ext_r[sweep][high, 0:FT],
             ],
             axis=0,
         )
@@ -371,6 +394,22 @@
             def _():
                 a_copy(sweep, step).start()
 
+    def rest_of_sweep(sweep):
+        order = order_of(sweep)
+        for c in range(CC):
+            moved = pltpu.roll(t_v[c], shift_of(sweep, 1), 1)
+            before = jnp.where(blocks(FT) == order[0], 0.0, moved).astype(BF16)
+            y = nn(d_in(sweep, c).reshape(NP * NUP, FT), before)
+            v_v[c] = v_v[c] - by_plane(NUP, y)
+        for step in (1, 2):
+
+            @pl.when(m_takes(sweep, step))
+            def _():
+                m_copy(sweep, step).wait_recv()
+
+        for c in range(CC):
+            mm_v[c] = nn(m_r[sweep, 0, c], m_r[sweep, 1, c]).astype(BF16)
+
     def take_ends(sweep):
         for step in (1, 2, 3):
 
@@ -378,36 +417,23 @@
             def _():
                 a_copy(sweep, step).wait_recv()
 
-        for step in (1, 2):
-
-            @pl.when(m_takes(sweep, step))
-            def _():
-                m_copy(sweep, step).wait_recv()
-
     def incoming(sweep, g):
         lanes = slice(LANES * g, LANES * g + LANES)
-
-        def applied(step, ends):
-            return by_block(FT, [(b, nn(m_r[sweep, step, 4 * g + b], ends)) for b in range(4)])
-
-        mid = a_r[sweep, 1, :, lanes].astype(F32) + applied(1, a_r[sweep, 2, :, lanes])
-        return a_r[sweep, 0, :, lanes].astype(F32) + applied(0, mid.astype(BF16))
+        parts = []
+        for b in range(4):
+            c = 4 * g + b
+            one = nn(m_r[sweep, 0, c], a_r[sweep, 1, :, lanes])
+            parts.append((b, one + nn(mm_v[c], a_r[sweep, 2, :, lanes])))
+        return a_r[sweep, 0, :, lanes].astype(F32) + by_block(FT, parts)
 
     def corrected(sweep, c, b, entering):
-        order = order_of(sweep)
-        t = spread(b, entering)
-        z = nn(li_v[sweep, c], t.astype(BF16))
-        before = by_block(
-            FT, [(order[0], t)] + [(order[o], z[FT * (o - 1) : FT * o]) for o in (1, 2, 3)]
-        )
-        local_part = pltpu.roll(t_v[c], shift_of(sweep, 1), 1)
-        before = before + jnp.where(blocks(FT) == order[0], 0.0, local_part)
-        low = LOWER if sweep == 0 else 0
-        d = d_v[c].reshape(NP * NUP, LOWER + FT)[:, low : low + FT]
-        return v_v[c] - by_plane(NUP, nn(d, before.astype(BF16)))
-
-    for copy in halo(0):
-        copy.wait_recv()
+        t = spread(b, entering).astype(BF16)
+        return v_v[c] - by_plane(NUP, nn(e_v[sweep, c].reshape(NP * NUP, FT), t))
+
+    load_neigh.wait()
+    for part in range(CC // CHUNK):
+        for copy in halo(0, part):
+            copy.wait_recv()
 
     @pl.when(s < 3)
     def _():
@@ -426,22 +452,25 @@
             total = packed(0, b, now, total)
         a_s[0, :, LANES * g : LANES * g + LANES] = total.astype(BF16)
     send_ends(0)
+    rest_of_sweep(0)
     take_ends(0)
     for g in range(2):
         entering = incoming(0, g)
         for b in range(4):
             c = 4 * g + b
             middle = corrected(0, c, b, entering)
-            picked = nn(sel[0 : 4 * FT], middle[0:NU].astype(BF16)).astype(BF16)
-            ext_l[1][CC + c] = picked[0 : 2 * FT]
-            ext_r[1][c] = picked[2 * FT : 4 * FT]
+            picked = nn(sel[0 : 2 * WT, 0:NU], middle[0:NU].astype(BF16)).astype(BF16)
+            ext_l[1][CC + c] = picked[0:WT]
+            ext_r[1][c] = picked[WT : 2 * WT]
+            if c % CHUNK == CHUNK - 1:
+                for copy in halo(1, c // CHUNK):
+                    copy.start()
             w_v[c] = middle + x_v[c]
-    for copy in halo(1):
-        copy.start()
     sections(1)
 
-    for copy in halo(1):
-        copy.wait_recv()
+    for part in range(CC // CHUNK):
+        for copy in halo(1, part):
+            copy.wait_recv()
     nothing = jnp.zeros((FT, LANES), BF16)
     for g in range(2):
         total = jnp.zeros((FT, LANES), F32)
@@ -452,7 +481,12 @@
             total = packed(1, b, now, total)
         a_s[1, :, LANES * g : LANES * g + LANES] = total.astype(BF16)
     send_ends(1)
+    rest_of_sweep(1)
     take_ends(1)
+
+    def out_store(c):
+        return pltpu.make_async_copy(out_v.at[:, c], out_hbm.at[:, c], out_sem.at[c])
+
     same = (
         lax.broadcasted_iota(jnp.int32, (LANES, LANES), 0)
         == lax.broadcasted_iota(jnp.int32, (LANES, LANES), 1)
@@ -463,10 +497,14 @@
             c = 4 * g + b
             result = corrected(1, c, b, entering)[0:NU].astype(BF16)
             out_v[:, c] = nt(same, result).astype(BF16).reshape(NP, R, NU)
+            out_store(c).start()
+    for c in range(CC):
+        out_store(c).wait()
 
     for sweep in (0, 1):
-        for copy in halo(sweep):
-            copy.wait_send()
+        for part in range(CC // CHUNK):
+            for copy in halo(sweep, part):
+                copy.wait_send()
         for step in (1, 2, 3):
 
             @pl.when(a_sends(sweep, step))
@@ -492,15 +530,18 @@
         functools.partial(kernel, crosses),
         out_shape=jax.ShapeDtypeStruct(right_sides.shape, BF16),
         in_specs=[
-            pl.BlockSpec(memory_space=pltpu.SMEM),
-            pl.BlockSpec(memory_space=pltpu.VMEM),
+            hbm,
+            hbm,
             hbm,
             hbm,
             hbm,
             hbm,
         ],
-        out_specs=pl.BlockSpec(memory_space=pltpu.VMEM),
+        out_specs=pl.BlockSpec(memory_space=pl.ANY),
         scratch_shapes=[
+            pltpu.SMEM((4, CC), jnp.int32),
+            vmem((2 * WT + 3 * FT, NU), BF16),
+            vmem((NP, CC, R, NU), BF16),
             vmem((NP, CC, R, NU), BF16),
             vmem((NP, CC, R, NU), BF16),
             vmem((NP, NU, CC, NU), BF16),
@@ -519,21 +560,23 @@
             vmem((2, CC, 3 * FT, FT), BF16),
             vmem((2, CC, 2 * FT, FT), BF16),
             vmem((2, CC, FT, FT), BF16),
-            vmem((2, CC, 3 * FT, FT), BF16),
-            vmem((2 * CC, 2 * FT, LANES), BF16),
-            vmem((2 * CC, 2 * FT, LANES), BF16),
-            vmem((2 * CC, 2 * FT, LANES), BF16),
-            vmem((2 * CC, 2 * FT, LANES), BF16),
+            vmem((2, CC, NP, NUP, FT), BF16),
+            vmem((CC, FT, FT), BF16),
+            vmem((2 * CC, WT, LANES), BF16),
+            vmem((2 * CC, WT, LANES), BF16),
+            vmem((2 * CC, WT, LANES), BF16),
+            vmem((2 * CC, WT, LANES), BF16),
             vmem((FT, CC * R), BF16),
             vmem((FT, CC * R), BF16),
             vmem((2, FT, CC * R), BF16),
             vmem((2, 3, FT, CC * R), BF16),
             vmem((2, CC, FT, FT), BF16),
             vmem((2, 2, CC, FT, FT), BF16),
-            dma((2,)),
+            dma((4,)),
             dma((2, NP)),
-            dma((2, 2)),
-            dma((2, 2)),
+            dma((CC,)),
+            dma((2, 2, CC // CHUNK)),
+            dma((2, 2, CC // CHUNK)),
             dma((2,)),
             dma((2, 3)),
             dma((2, 3)),

time: 53.2 us -> 49.3 us (0.927)
  Pallas kernels: 51.2 us -> 47.3 us
    pallas_call x1, Pallas kernels: 51.2 us -> 47.3 us  [local(): pl.pallas_call(functools.partial(kernel, crosses), out_shape=jax.ShapeDty...]
where the time goes in v3:
time: 49.3 us; the launch traced here: 49.2 us
  Pallas kernels  47.3 us (96%)
  local copies, waits for them, and re-layouts  1.87 us (4%)
    pallas_call x1, Pallas kernels, local(): pl.pallas_call(functools.partial(kernel, crosses), out_shape=jax.ShapeDty...  47.3 us
    unnamed x1, local copies, waits for them, and re-layouts  1.87 us

profile of v3, /device:TPU:1, one launch (start us, length us, event | category | flops | bytes accessed | tf_op | source)
XLA Modules:
  0.0 49.2 jit_solution(12008798916793532506)
XLA Ops:
  0.0 47.3 %sweeps.1 = bf16[4,8,32,135]{3,2,1,0:T(8,128)(2,1)} custom-call(s32[4,8]{1,0:T(4,128)} %bitcast.5, bf16[304,135]{1,0:T(8,128)(2,1)} %constant.2.clone.sel_hbm, bf16[4,8,32,135]{3,2,1,0:T(8,128)(2,1)} %rhs_hbm.1, bf16[4,8,32,135]{3,2,1,0:T(8,128)(2,1)} %init_hbm.1, bf16[4,135,8,135]{3,2,1,0:T(8,128)(2,1)} %bitcast.4, bf16[4,6,45,8,135]{4,3,2,1,0:T(8,128)(2,1)} %bitcast.3), custom_call_target="tpu_custom_call" | custom-call | tf_op jit(solution)/shard_map/sweeps/pallas_call | solution.py:529
  47.3 1.9 %copy.8 = bf16[4,8,32,135]{3,2,1,0:T(8,128)(2,1)} copy(bf16[4,8,32,135]{3,2,1,0:T(8,128)(2,1)} %sweeps.1) | data formatting | bytes 552960

commit v4 on v3

--- a/solution.py
+++ b/solution.py
@@ -87,6 +87,10 @@
     t_v,
     us_v,
     q_v,
+    face_v,
+    col_v,
+    u_v,
+    w_face_v,
     l1_v,
     l2_v,
     l3_v,
@@ -255,6 +259,8 @@
         stack_v[:, :, top + 32 : top + FT] = jnp.zeros((CC, NP, 16, NU), BF16)
     stack_v[:, :, NSTACK:LOWER] = jnp.zeros((CC, NP, LOWER - NSTACK, NU), BF16)
     q_v[...] = jnp.zeros_like(q_v)
+    for rows in (u_v, w_face_v):
+        rows[:, 40:FT] = jnp.zeros((CC, FT - 40, LANES), F32)
 
     def turn(slot, block, count, to, p, first):
         flat = block.astype(F32).reshape(CC * count, NU)
@@ -284,12 +290,10 @@
         for c in range(CC):
             d = nt(inv_v[c, p], stack_v[c, p])
             d_v[c, p] = d.astype(BF16)
-            rows_v[0, c] = d[:, LOWER : LOWER + FT]
-            rows_v[1, c] = d[:, 0:FT]
+            rows_v[c] = d[:, LOWER : LOWER + FT]
             for var in range(5):
                 to = slice(9 * var, 9 * var + 9)
-                q_v[0, c, p, to] = rows_v[0, c, 27 * var + 18 : 27 * var + 27]
-                q_v[1, c, p, to] = rows_v[1, c, 27 * var : 27 * var + 9]
+                q_v[c, p, to] = rows_v[c, 27 * var + 18 : 27 * var + 27]
         return carry
 
     lax.fori_loop(0, NP, products, 0)
@@ -311,7 +315,10 @@
 
     def sections(sweep):
         order = order_of(sweep)
-        n = [[(-q_v[sweep, c, p]).astype(BF16) for p in order] for c in range(CC)]
+        if sweep == 0:
+            n = [[(-q_v[c, p]).astype(BF16) for p in order] for c in range(CC)]
+        else:
+            n = [[-face_v[c, p, :, 0:FT] for p in order] for c in range(CC)]
         two = [
             [nn(n[c][o], n[c][o - 1]).astype(BF16) for o in (1, 2, 3)] for c in range(CC)
         ]
@@ -340,42 +347,40 @@
         low = jnp.clip(low, 0, 2 * CC - 1)
         high = jnp.clip(high, 0, 2 * CC - 1)
         apart = [sel[2 * WT + FT * half : 2 * WT + FT * half + FT, 0:WT] for half in (1, 2)]
-        return jnp.concatenate(
-            [
-                upper,
-                nn(apart[0], ext_l[sweep][c]).astype(BF16),
-                nn(apart[1], ext_r[sweep][CC + c]).astype(BF16),
-                ext_l[sweep][low, 0:FT],
-                ext_r[sweep][high, 0:FT],
-            ],
-            axis=0,
-        )
+        col_v[c, 0:FT] = upper
+        col_v[c, FT : 2 * FT] = nn(apart[0], ext_l[sweep][c]).astype(BF16)
+        col_v[c, 2 * FT : 3 * FT] = nn(apart[1], ext_r[sweep][CC + c]).astype(BF16)
+        col_v[c, 3 * FT : 4 * FT] = ext_l[sweep][low, 0:FT]
+        col_v[c, 4 * FT : 5 * FT] = ext_r[sweep][high, 0:FT]
 
     def shift_of(sweep, steps):
         return R * steps if sweep == 0 else LANES - R * steps
 
-    def local_sweep(sweep, c, base, upper):
+    def applied_to_column(c):
+        d = d_v[c].reshape(NP * NUP, LOWER + FT)[:, 0:NSTACK]
+        return by_plane(NUP, nn(d, col_v[c]))
+
+    def local_faces(sweep):
         order = order_of(sweep)
-        stack = gathered(sweep, c, upper)
-        x = by_plane(NUP, nn(d_v[c].reshape(NP * NUP, LOWER + FT)[:, 0:NSTACK], stack))
-        v = base - x
-        v_v[c] = v
-        if sweep == 0:
-            x_v[c] = x
-        start = 18 if sweep == 0 else 0
-        pieces = [v_v[c, 27 * var + start : 27 * var + start + 9] for var in range(5)]
-        for var in range(5):
-            t_v[c, 9 * var : 9 * var + 9] = pieces[var]
-        u = t_v[c]
         block = blocks(FT)
-        total = u
-        for steps, left_v in ((1, l1_v), (2, l2_v), (3, l3_v)):
-            moved = pltpu.roll(u, shift_of(sweep, steps), 1).astype(BF16)
-            z = nn(left_v[sweep, c], moved)
-            for o in range(steps, NP):
-                part = z[FT * (o - steps) : FT * (o - steps + 1)]
-                total = total + jnp.where(block == order[o], part, 0.0)
-        return total
+        for c in range(CC):
+            total = u_v[c]
+            for steps, left_v in ((1, l1_v), (2, l2_v), (3, l3_v)):
+                moved = pltpu.roll(u_v[c], shift_of(sweep, steps), 1).astype(BF16)
+                z = nn(left_v[sweep, c], moved)
+                for o in range(steps, NP):
+                    part = z[FT * (o - steps) : FT * (o - steps + 1)]
+                    total = total + jnp.where(block == order[o], part, 0.0)
+            t_v[c] = total
+        for g in range(2):
+            total = jnp.zeros((FT, LANES), F32)
+            for b in range(4):
+                total = packed(sweep, b, t_v[4 * g + b], total)
+            a_s[sweep, :, LANES * g : LANES * g + LANES] = total.astype(BF16)
+
+    def before_of(sweep, c):
+        moved = pltpu.roll(t_v[c], shift_of(sweep, 1), 1)
+        return jnp.where(blocks(FT) == order_of(sweep)[0], 0.0, moved).astype(BF16)
 
     def packed(sweep, b, now, total):
         last = 3 if sweep == 0 else 0
@@ -394,13 +399,7 @@
             def _():
                 a_copy(sweep, step).start()
 
-    def rest_of_sweep(sweep):
-        order = order_of(sweep)
-        for c in range(CC):
-            moved = pltpu.roll(t_v[c], shift_of(sweep, 1), 1)
-            before = jnp.where(blocks(FT) == order[0], 0.0, moved).astype(BF16)
-            y = nn(d_in(sweep, c).reshape(NP * NUP, FT), before)
-            v_v[c] = v_v[c] - by_plane(NUP, y)
+    def take_operators(sweep):
         for step in (1, 2):
 
             @pl.when(m_takes(sweep, step))
@@ -439,20 +438,23 @@
     def _():
         up_copy.wait_recv()
 
-    t_v[...] = jnp.zeros_like(t_v)
-    for g in range(2):
-        total = jnp.zeros((FT, LANES), F32)
-        for b in range(4):
-            c = 4 * g + b
-            edge = up_r[:, LANES * g : LANES * g + LANES].astype(F32)
-            edge = pltpu.roll(edge, (R * (3 - b)) % LANES, 1) if b != 3 else edge
-            upper = jnp.where(blocks(FT) == 3, edge, us_v[c]).astype(BF16)
-            now = local_sweep(0, c, w_v[c], upper)
-            t_v[c] = now
-            total = packed(0, b, now, total)
-        a_s[0, :, LANES * g : LANES * g + LANES] = total.astype(BF16)
+    for c in range(CC):
+        g, b = c // 4, c % 4
+        edge = up_r[:, LANES * g : LANES * g + LANES].astype(F32)
+        edge = pltpu.roll(edge, (R * (3 - b)) % LANES, 1) if b != 3 else edge
+        gathered(0, c, jnp.where(blocks(FT) == 3, edge, us_v[c]).astype(BF16))
+    for c in range(CC):
+        x = applied_to_column(c)
+        x_v[c] = x
+        v_v[c] = w_v[c] - x
+        for var in range(5):
+            u_v[c, 9 * var : 9 * var + 9] = v_v[c, 27 * var + 18 : 27 * var + 27]
+    local_faces(0)
     send_ends(0)
-    rest_of_sweep(0)
+    for c in range(CC):
+        y = nn(d_in(0, c).reshape(NP * NUP, FT), before_of(0, c))
+        v_v[c] = v_v[c] - by_plane(NUP, y)
+    take_operators(0)
     take_ends(0)
     for g in range(2):
         entering = incoming(0, g)
@@ -466,22 +468,28 @@
                 for copy in halo(1, c // CHUNK):
                     copy.start()
             w_v[c] = middle + x_v[c]
+    for c in range(CC):
+        for p in range(NP):
+            face_v[c, p] = nn(sel[2 * WT : 2 * WT + FT], d_v[c, p, 0:NU, 0:NSTACK]).astype(BF16)
+        for var in range(5):
+            w_face_v[c, 9 * var : 9 * var + 9] = w_v[c, 27 * var : 27 * var + 9]
     sections(1)
 
     for part in range(CC // CHUNK):
         for copy in halo(1, part):
             copy.wait_recv()
-    nothing = jnp.zeros((FT, LANES), BF16)
-    for g in range(2):
-        total = jnp.zeros((FT, LANES), F32)
-        for b in range(4):
-            c = 4 * g + b
-            now = local_sweep(1, c, w_v[c], nothing)
-            t_v[c] = now
-            total = packed(1, b, now, total)
-        a_s[1, :, LANES * g : LANES * g + LANES] = total.astype(BF16)
+    for c in range(CC):
+        gathered(1, c, jnp.zeros((FT, LANES), BF16))
+    for c in range(CC):
+        faces = face_v[c].reshape(NP * FT, NSTACK)
+        u_v[c] = w_face_v[c] - by_plane(FT, nn(faces, col_v[c]))
+    local_faces(1)
     send_ends(1)
-    rest_of_sweep(1)
+    for c in range(CC):
+        col_v[c, 0:FT] = before_of(1, c)
+    for c in range(CC):
+        v_v[c] = w_v[c] - applied_to_column(c)
+    take_operators(1)
     take_ends(1)
 
     def out_store(c):
@@ -550,13 +558,17 @@
             vmem((CC, NP, NUP, NU), BF16),
             vmem((CC, NP, LOWER + FT, NU), BF16),
             vmem((CC, NP, NUP, LOWER + FT), BF16),
-            vmem((2, CC, NUP, FT), F32),
+            vmem((CC, NUP, FT), F32),
             vmem((CC, NUP, LANES), F32),
             vmem((CC, NUP, LANES), F32),
             vmem((CC, NUP, LANES), F32),
             vmem((CC, FT, LANES), F32),
             vmem((CC, FT, LANES), F32),
-            vmem((2, CC, NP, FT, FT), F32),
+            vmem((CC, NP, FT, FT), F32),
+            vmem((CC, NP, FT, NSTACK), BF16),
+            vmem((CC, NSTACK, LANES), BF16),
+            vmem((CC, FT, LANES), F32),
+            vmem((CC, FT, LANES), F32),
             vmem((2, CC, 3 * FT, FT), BF16),
             vmem((2, CC, 2 * FT, FT), BF16),
             vmem((2, CC, FT, FT), BF16),

time: 49.3 us -> 44.3 us (0.90)
  Pallas kernels: 47.3 us -> 42.1 us
    pallas_call x1, Pallas kernels: 47.3 us -> 42.1 us  [local(): pl.pallas_call(functools.partial(kernel, crosses), out_shape=jax.ShapeDty...]
where the time goes in v4:
time: 44.3 us; the launch traced here: 44 us
  Pallas kernels  42.1 us (95%)
  local copies, waits for them, and re-layouts  1.87 us (4%)
    pallas_call x1, Pallas kernels, local(): pl.pallas_call(functools.partial(kernel, crosses), out_shape=jax.ShapeDty...  42.1 us
    unnamed x1, local copies, waits for them, and re-layouts  1.87 us

profile of v4, /device:TPU:1, one launch (start us, length us, event | category | flops | bytes accessed | tf_op | source)
XLA Modules:
  0.0 44.0 jit_solution(4128927656526881335)
XLA Ops:
  0.0 42.1 %sweeps.1 = bf16[4,8,32,135]{3,2,1,0:T(8,128)(2,1)} custom-call(s32[4,8]{1,0:T(4,128)} %bitcast.5, bf16[304,135]{1,0:T(8,128)(2,1)} %constant.2.clone.sel_hbm, bf16[4,8,32,135]{3,2,1,0:T(8,128)(2,1)} %rhs_hbm.1, bf16[4,8,32,135]{3,2,1,0:T(8,128)(2,1)} %init_hbm.1, bf16[4,135,8,135]{3,2,1,0:T(8,128)(2,1)} %bitcast.4, bf16[4,6,45,8,135]{4,3,2,1,0:T(8,128)(2,1)} %bitcast.3), custom_call_target="tpu_custom_call" | custom-call | tf_op jit(solution)/shard_map/sweeps/pallas_call | solution.py:537
  42.1 1.9 %copy.8 = bf16[4,8,32,135]{3,2,1,0:T(8,128)(2,1)} copy(bf16[4,8,32,135]{3,2,1,0:T(8,128)(2,1)} %sweeps.1) | data formatting | bytes 552960

commit v5 on v4

--- a/solution.py
+++ b/solution.py
@@ -94,6 +94,7 @@
     l1_v,
     l2_v,
     l3_v,
+    li_v,
     e_v,
     mm_v,
     ext_l0,
@@ -273,30 +274,33 @@
                 :, 0 : NU - 128
             ].astype(BF16)
 
-    def products(p, carry):
+    def turns(p):
+        steps = []
+        for first in range(0, NU, 16):
+            steps.append((inv_n, (p,), inv_v, 0, first, min(16, NU - first)))
+        for top, face in [(FT * place, face) for place, face in enumerate(STACK)] + [(LOWER, 0)]:
+            for first in range(0, NT, 16):
+                steps.append((cpl_n, (p, face), stack_v, top, first, min(16, NT - first)))
+        return steps
+
+    def product(p, c):
+        d = nt(inv_v[c, p], stack_v[c, p])
+        d_v[c, p] = d.astype(BF16)
+        rows_v[c] = d[:, LOWER : LOWER + FT]
+        for var in range(5):
+            to = slice(9 * var, 9 * var + 9)
+            q_v[c, p, to] = rows_v[c, 27 * var + 18 : 27 * var + 27]
+
+    for p in range(NP):
         inv_load(p).wait()
         cpl_load(p).wait()
-        slot = 0
-        for first in range(0, NU, 16):
-            count = min(16, NU - first)
-            turn(slot, inv_n[p, first : first + count], count, inv_v, p, first)
-            slot += 1
-        for top, face in [(FT * place, face) for place, face in enumerate(STACK)] + [(LOWER, 0)]:
-            for first in range(0, NT, 16):
-                count = min(16, NT - first)
-                block = cpl_n[p, face, first : first + count]
-                turn(slot, block, count, stack_v, p, top + first)
-                slot += 1
-        for c in range(CC):
-            d = nt(inv_v[c, p], stack_v[c, p])
-            d_v[c, p] = d.astype(BF16)
-            rows_v[c] = d[:, LOWER : LOWER + FT]
-            for var in range(5):
-                to = slice(9 * var, 9 * var + 9)
-                q_v[c, p, to] = rows_v[c, 27 * var + 18 : 27 * var + 27]
-        return carry
-
-    lax.fori_loop(0, NP, products, 0)
+        for slot, (source, at, to, top, first, count) in enumerate(turns(p)):
+            block = source[at + (slice(first, first + count),)]
+            turn(slot, block, count, to, p, top + first)
+            if p > 0 and slot % 3 == 0 and slot // 3 < CC:
+                product(p - 1, slot // 3)
+    for c in range(CC):
+        product(NP - 1, c)
     load_rhs.wait()
 
     def by_plane(rows, stacked):
@@ -327,10 +331,8 @@
                 l1_v[sweep, c, FT * (o - 1) : FT * o] = n[c][o]
             for o in (2, 3):
                 l2_v[sweep, c, FT * (o - 2) : FT * (o - 1)] = two[c][o - 1]
-            e_v[sweep, c, order[0]] = d_in(sweep, c)[order[0]]
-            fronts = (n[c][0], two[c][0], nn(two[c][1], n[c][0]).astype(BF16))
-            for o in (1, 2, 3):
-                e_v[sweep, c, order[o]] = nn(d_in(sweep, c)[order[o]], fronts[o - 1]).astype(BF16)
+            li_v[c, 0] = n[c][0]
+            li_v[c, 1] = two[c][0]
             l3_v[sweep, c] = nn(two[c][2], n[c][1]).astype(BF16)
             m_s[sweep, c] = nn(two[c][2], two[c][0]).astype(BF16)
         for step in (1, 2):
@@ -340,6 +342,15 @@
                 m_copy(sweep, step).start()
 
     sections(0)
+
+    def fronts_applied(sweep):
+        order = order_of(sweep)
+        for c in range(CC):
+            first = li_v[c, 0]
+            fronts = (first, li_v[c, 1], nn(l2_v[sweep, c, 0:FT], first).astype(BF16))
+            e_v[sweep, c, order[0]] = d_in(sweep, c)[order[0]]
+            for o in (1, 2, 3):
+                e_v[sweep, c, order[o]] = nn(d_in(sweep, c)[order[o]], fronts[o - 1]).astype(BF16)
 
     def gathered(sweep, c, upper):
         low = lax.rem(neigh[2, c] - (k - 1) * CC + 2 * crosses * CC, crosses * CC)
@@ -451,6 +462,7 @@
             u_v[c, 9 * var : 9 * var + 9] = v_v[c, 27 * var + 18 : 27 * var + 27]
     local_faces(0)
     send_ends(0)
+    fronts_applied(0)
     for c in range(CC):
         y = nn(d_in(0, c).reshape(NP * NUP, FT), before_of(0, c))
         v_v[c] = v_v[c] - by_plane(NUP, y)
@@ -474,6 +486,7 @@
         for var in range(5):
             w_face_v[c, 9 * var : 9 * var + 9] = w_v[c, 27 * var : 27 * var + 9]
     sections(1)
+    fronts_applied(1)
 
     for part in range(CC // CHUNK):
         for copy in halo(1, part):
@@ -572,6 +585,7 @@
             vmem((2, CC, 3 * FT, FT), BF16),
             vmem((2, CC, 2 * FT, FT), BF16),
             vmem((2, CC, FT, FT), BF16),
+            vmem((CC, 2, FT, FT), BF16),
             vmem((2, CC, NP, NUP, FT), BF16),
             vmem((CC, FT, FT), BF16),
             vmem((2 * CC, WT, LANES), BF16),

time: 44.3 us -> 44.5 us (level)
  no operation moved by 1% of the time
where the time goes in v5:
time: 44.5 us; the launch traced here: 44 us
  Pallas kernels  42.1 us (95%)
  local copies, waits for them, and re-layouts  1.87 us (4%)
    pallas_call x1, Pallas kernels, local(): pl.pallas_call(functools.partial(kernel, crosses), out_shape=jax.ShapeDty...  42.1 us
    unnamed x1, local copies, waits for them, and re-layouts  1.87 us

profile of v5, /device:TPU:1, one launch (start us, length us, event | category | flops | bytes accessed | tf_op | source)
XLA Modules:
  0.0 44.0 jit_solution(8273984455456459712)
XLA Ops:
  0.0 42.1 %sweeps.1 = bf16[4,8,32,135]{3,2,1,0:T(8,128)(2,1)} custom-call(s32[4,8]{1,0:T(4,128)} %bitcast.5, bf16[304,135]{1,0:T(8,128)(2,1)} %constant.2.clone.sel_hbm, bf16[4,8,32,135]{3,2,1,0:T(8,128)(2,1)} %rhs_hbm.1, bf16[4,8,32,135]{3,2,1,0:T(8,128)(2,1)} %init_hbm.1, bf16[4,135,8,135]{3,2,1,0:T(8,128)(2,1)} %bitcast.4, bf16[4,6,45,8,135]{4,3,2,1,0:T(8,128)(2,1)} %bitcast.3), custom_call_target="tpu_custom_call" | custom-call | tf_op jit(solution)/shard_map/sweeps/pallas_call | solution.py:550
  42.1 1.9 %copy.8 = bf16[4,8,32,135]{3,2,1,0:T(8,128)(2,1)} copy(bf16[4,8,32,135]{3,2,1,0:T(8,128)(2,1)} %sweeps.1) | data formatting | bytes 552960

commit v6 on v4

--- a/solution.py
+++ b/solution.py
@@ -94,6 +94,7 @@
     l1_v,
     l2_v,
     l3_v,
+    li_v,
     e_v,
     mm_v,
     ext_l0,
@@ -327,10 +328,8 @@
                 l1_v[sweep, c, FT * (o - 1) : FT * o] = n[c][o]
             for o in (2, 3):
                 l2_v[sweep, c, FT * (o - 2) : FT * (o - 1)] = two[c][o - 1]
-            e_v[sweep, c, order[0]] = d_in(sweep, c)[order[0]]
-            fronts = (n[c][0], two[c][0], nn(two[c][1], n[c][0]).astype(BF16))
-            for o in (1, 2, 3):
-                e_v[sweep, c, order[o]] = nn(d_in(sweep, c)[order[o]], fronts[o - 1]).astype(BF16)
+            li_v[c, 0] = n[c][0]
+            li_v[c, 1] = two[c][0]
             l3_v[sweep, c] = nn(two[c][2], n[c][1]).astype(BF16)
             m_s[sweep, c] = nn(two[c][2], two[c][0]).astype(BF16)
         for step in (1, 2):
@@ -340,6 +339,15 @@
                 m_copy(sweep, step).start()
 
     sections(0)
+
+    def fronts_applied(sweep):
+        order = order_of(sweep)
+        for c in range(CC):
+            first = li_v[c, 0]
+            fronts = (first, li_v[c, 1], nn(l2_v[sweep, c, 0:FT], first).astype(BF16))
+            e_v[sweep, c, order[0]] = d_in(sweep, c)[order[0]]
+            for o in (1, 2, 3):
+                e_v[sweep, c, order[o]] = nn(d_in(sweep, c)[order[o]], fronts[o - 1]).astype(BF16)
 
     def gathered(sweep, c, upper):
         low = lax.rem(neigh[2, c] - (k - 1) * CC + 2 * crosses * CC, crosses * CC)
@@ -451,6 +459,7 @@
             u_v[c, 9 * var : 9 * var + 9] = v_v[c, 27 * var + 18 : 27 * var + 27]
     local_faces(0)
     send_ends(0)
+    fronts_applied(0)
     for c in range(CC):
         y = nn(d_in(0, c).reshape(NP * NUP, FT), before_of(0, c))
         v_v[c] = v_v[c] - by_plane(NUP, y)
@@ -474,6 +483,7 @@
         for var in range(5):
             w_face_v[c, 9 * var : 9 * var + 9] = w_v[c, 27 * var : 27 * var + 9]
     sections(1)
+    fronts_applied(1)
 
     for part in range(CC // CHUNK):
         for copy in halo(1, part):
@@ -572,6 +582,7 @@
             vmem((2, CC, 3 * FT, FT), BF16),
             vmem((2, CC, 2 * FT, FT), BF16),
             vmem((2, CC, FT, FT), BF16),
+            vmem((CC, 2, FT, FT), BF16),
             vmem((2, CC, NP, NUP, FT), BF16),
             vmem((CC, FT, FT), BF16),
             vmem((2 * CC, WT, LANES), BF16),

time: 44.3 us -> 44.2 us (level)
  no operation moved by 1% of the time
where the time goes in v6:
time: 44.2 us; the launch traced here: 43.8 us
  Pallas kernels  41.9 us (95%)
  local copies, waits for them, and re-layouts  1.87 us (4%)
    pallas_call x1, Pallas kernels, local(): pl.pallas_call(functools.partial(kernel, crosses), out_shape=jax.ShapeDty...  41.9 us
    unnamed x1, local copies, waits for them, and re-layouts  1.87 us

profile of v6, /device:TPU:1, one launch (start us, length us, event | category | flops | bytes accessed | tf_op | source)
XLA Modules:
  0.0 43.8 jit_solution(939078907125975143)
XLA Ops:
  0.0 41.9 %sweeps.1 = bf16[4,8,32,135]{3,2,1,0:T(8,128)(2,1)} custom-call(s32[4,8]{1,0:T(4,128)} %bitcast.5, bf16[304,135]{1,0:T(8,128)(2,1)} %constant.2.clone.sel_hbm, bf16[4,8,32,135]{3,2,1,0:T(8,128)(2,1)} %rhs_hbm.1, bf16[4,8,32,135]{3,2,1,0:T(8,128)(2,1)} %init_hbm.1, bf16[4,135,8,135]{3,2,1,0:T(8,128)(2,1)} %bitcast.4, bf16[4,6,45,8,135]{4,3,2,1,0:T(8,128)(2,1)} %bitcast.3), custom_call_target="tpu_custom_call" | custom-call | tf_op jit(solution)/shard_map/sweeps/pallas_call | solution.py:547
  41.9 1.9 %copy.8 = bf16[4,8,32,135]{3,2,1,0:T(8,128)(2,1)} copy(bf16[4,8,32,135]{3,2,1,0:T(8,128)(2,1)} %sweeps.1) | data formatting | bytes 552960

commit v7 on v6

--- a/solution.py
+++ b/solution.py
@@ -18,7 +18,7 @@
 STACK = (1, 2, 3, 4, 5)
 NSTACK = len(STACK) * FT
 LOWER = 256
-CHUNK = 2
+CHUNK = 1
 
 
 def selector():

time: 44.2 us -> 44.1 us (level)
  no operation moved by 1% of the time
where the time goes in v7:
time: 44.1 us; the launch traced here: 44 us
  Pallas kernels  42.1 us (95%)
  local copies, waits for them, and re-layouts  1.87 us (4%)
    pallas_call x1, Pallas kernels, local(): pl.pallas_call(functools.partial(kernel, crosses), out_shape=jax.ShapeDty...  42.1 us
    unnamed x1, local copies, waits for them, and re-layouts  1.87 us

profile of v7, /device:TPU:1, one launch (start us, length us, event | category | flops | bytes accessed | tf_op | source)
XLA Modules:
  0.0 44.0 jit_solution(8993151719110949458)
XLA Ops:
  0.0 42.1 %sweeps.1 = bf16[4,8,32,135]{3,2,1,0:T(8,128)(2,1)} custom-call(s32[4,8]{1,0:T(4,128)} %bitcast.5, bf16[304,135]{1,0:T(8,128)(2,1)} %constant.2.clone.sel_hbm, bf16[4,8,32,135]{3,2,1,0:T(8,128)(2,1)} %rhs_hbm.1, bf16[4,8,32,135]{3,2,1,0:T(8,128)(2,1)} %init_hbm.1, bf16[4,135,8,135]{3,2,1,0:T(8,128)(2,1)} %bitcast.4, bf16[4,6,45,8,135]{4,3,2,1,0:T(8,128)(2,1)} %bitcast.3), custom_call_target="tpu_custom_call" | custom-call | tf_op jit(solution)/shard_map/sweeps/pallas_call | solution.py:547
  42.1 1.9 %copy.8 = bf16[4,8,32,135]{3,2,1,0:T(8,128)(2,1)} copy(bf16[4,8,32,135]{3,2,1,0:T(8,128)(2,1)} %sweeps.1) | data formatting | bytes 552960

commit v8 on v6

--- a/solution.py
+++ b/solution.py
@@ -176,6 +176,15 @@
         device_id_type=MESH,
     )
 
+    inv_v[:, :, NU - 7 : NUP] = jnp.zeros((CC, NP, NUP - NU + 7, NU), BF16)
+    for place in list(range(len(STACK))) + [LOWER // FT]:
+        top = LOWER if place == LOWER // FT else FT * place
+        stack_v[:, :, top + 32 : top + FT] = jnp.zeros((CC, NP, 16, NU), BF16)
+    stack_v[:, :, NSTACK:LOWER] = jnp.zeros((CC, NP, LOWER - NSTACK, NU), BF16)
+    q_v[...] = jnp.zeros_like(q_v)
+    for rows in (u_v, w_face_v):
+        rows[:, 40:FT] = jnp.zeros((CC, FT - 40, LANES), F32)
+
     load_sel.wait()
     load_init.wait()
     up_s[...] = nt(sel[2 * WT : 2 * WT + FT], init_v[0].reshape(CC * R, NU)).astype(BF16)
@@ -253,15 +262,6 @@
         @pl.when(s + step > 2)
         def _():
             m_r[1, step - 1] = jnp.zeros((CC, FT, FT), BF16)
-
-    inv_v[:, :, NU - 7 : NUP] = jnp.zeros((CC, NP, NUP - NU + 7, NU), BF16)
-    for place in list(range(len(STACK))) + [LOWER // FT]:
-        top = LOWER if place == LOWER // FT else FT * place
-        stack_v[:, :, top + 32 : top + FT] = jnp.zeros((CC, NP, 16, NU), BF16)
-    stack_v[:, :, NSTACK:LOWER] = jnp.zeros((CC, NP, LOWER - NSTACK, NU), BF16)
-    q_v[...] = jnp.zeros_like(q_v)
-    for rows in (u_v, w_face_v):
-        rows[:, 40:FT] = jnp.zeros((CC, FT - 40, LANES), F32)
 
     def turn(slot, block, count, to, p, first):
         flat = block.astype(F32).reshape(CC * count, NU)

time: 44.2 us -> 43.8 us (level)
  no operation moved by 1% of the time
where the time goes in v8:
time: 43.8 us; the launch traced here: 43.4 us
  Pallas kernels  41.5 us (95%)
  local copies, waits for them, and re-layouts  1.87 us (4%)
    pallas_call x1, Pallas kernels, local(): pl.pallas_call(functools.partial(kernel, crosses), out_shape=jax.ShapeDty...  41.5 us
    unnamed x1, local copies, waits for them, and re-layouts  1.87 us

profile of v8, /device:TPU:1, one launch (start us, length us, event | category | flops | bytes accessed | tf_op | source)
XLA Modules:
  0.0 43.4 jit_solution(2869278595605524021)
XLA Ops:
  0.0 41.5 %sweeps.1 = bf16[4,8,32,135]{3,2,1,0:T(8,128)(2,1)} custom-call(s32[4,8]{1,0:T(4,128)} %bitcast.5, bf16[304,135]{1,0:T(8,128)(2,1)} %constant.2.clone.sel_hbm, bf16[4,8,32,135]{3,2,1,0:T(8,128)(2,1)} %rhs_hbm.1, bf16[4,8,32,135]{3,2,1,0:T(8,128)(2,1)} %init_hbm.1, bf16[4,135,8,135]{3,2,1,0:T(8,128)(2,1)} %bitcast.4, bf16[4,6,45,8,135]{4,3,2,1,0:T(8,128)(2,1)} %bitcast.3), custom_call_target="tpu_custom_call" | custom-call | tf_op jit(solution)/shard_map/sweeps/pallas_call | solution.py:547
  41.5 1.9 %copy.8 = bf16[4,8,32,135]{3,2,1,0:T(8,128)(2,1)} copy(bf16[4,8,32,135]{3,2,1,0:T(8,128)(2,1)} %sweeps.1) | data formatting | bytes 552960
